TPU v7x, 32 devices: a whole 2x2x4 slice. The times are simulated.
32 devices in a mesh: layer: 2 (over x), expert: 4 (over y, core), col: 4 (over z).
Axes of the slice: x: 2, y: 2, z: 4, core: 2. Of those that a mesh axis runs over, the one named last changes fastest.
Arguments:
- target_weights: bfloat16 [8, 7168, 2048], P(('layer', 'expert'), None, 'col'), parts along dimension 0, may hold values from -36 to 36
- factors: float32 [8, 7168, 128], P(('layer', 'expert'), 'col'), parts along dimension 0, may hold values from -0.5 to 0.5
- bases: float32 [64, 128, 2048], P('layer', None, 'col'), parts along dimension 0, may hold values from -6 to 6
- coefficients: float32 [8, 32], P(('layer', 'expert')), parts along dimension 0, may hold values from -1 to 1
Outputs:
- new_factors: float32 [8, 7168, 128], P(('layer', 'expert'), 'col'), parts along dimension 0
- new_bases: float32 [64, 128, 2048], P('layer', None, 'col'), parts along dimension 0
- new_coefficients: float32 [8, 32], P(('layer', 'expert')), parts along dimension 0
- losses: float32 [4], P('layer'), parts along dimension 0
There are 2 independent parts, one for each index of `layer`. A program takes and returns all parts, laid end to end along the dimension named above; each array names one. Nothing has to cross between parts.
All inputs are finite; a program needn't handle non-finite values.
Results may differ from a plain program's by a relative error of at most 0.0003.
Values sent between devices are 32-bit elements; how exact they have to be, the bound alone decides.
A program may use at most 128 MiB of HBM per device.

v0:
```python
import functools

import jax
import jax.numpy as jnp
from jax import lax
from jax.experimental import pallas as pl
from jax.experimental.pallas import tpu as pltpu
from jax.sharding import PartitionSpec as P

LEARN_RATE = 0.01
BETA_ONE = 0.9
BETA_TWO = 0.999
EPSILON = 0.0001
HIGHEST = lax.Precision.HIGHEST
MESH = pl.DeviceIdType.MESH
F32 = jnp.float32
BF16 = jnp.bfloat16


def adam_first(parameter, g):
    return parameter - LEARN_RATE * g / (jnp.abs(g) + EPSILON)


def adam_second(parameter, g_one, g_two):
    first = (BETA_ONE * (1.0 - BETA_ONE) * g_one + (1.0 - BETA_ONE) * g_two) * (1.0 / (1.0 - BETA_ONE**2))
    second = (
        BETA_TWO * (1.0 - BETA_TWO) * g_one * g_one + (1.0 - BETA_TWO) * g_two * g_two
    ) * (1.0 / (1.0 - BETA_TWO**2))
    return parameter - LEARN_RATE * first / (jnp.sqrt(second) + EPSILON)


def pieces(x, count=3):
    out = []
    for _ in range(count):
        piece = x.astype(BF16)
        out.append(piece)
        x = x - piece.astype(F32)
    return out


def contract(a, b, dims):
    return lax.dot_general(a, b, (dims, ((), ())), preferred_element_type=F32)


def fold(x, r):
    return x[:, :r] + x[:, r : 2 * r] + x[:, 2 * r :]


def fold_rows(x, r):
    return x[:r] + x[r : 2 * r] + x[2 * r :]


def kernel(
    n, experts, t_hbm, f_hbm, b_hbm, c_in, f_out, b_out, c_out, l_out,
    target, bases, full, part, landed, d_pre, c_one, c_two, d_coef, loss_in, g_one, gram_sum,
    mixed, mixed_cut, loss_sum, load_sem, ag_send, ag_recv, rs_send, rs_recv, ex_send, ex_recv, co_send, co_recv,
):
    me = lax.axis_index("col")
    mine = lax.axis_index("expert")
    rows, r = f_out.shape
    d, hl = target.shape
    k_count = bases.shape[0]
    scale = 1.0 / (hl * n)
    table = experts * k_count

    loads = [
        pltpu.make_async_copy(f_hbm, full.at[0, pl.ds(pl.multiple_of(me * rows, 8), rows)], load_sem.at[0]),
        pltpu.make_async_copy(b_hbm, bases, load_sem.at[1]),
        pltpu.make_async_copy(t_hbm, target, load_sem.at[2]),
        pltpu.make_async_copy(c_in, c_one.at[mine], load_sem.at[3]),
    ]
    for load in loads:
        load.start()
    barrier = pltpu.get_barrier_semaphore()
    for off in range(1, n):
        pl.semaphore_signal(barrier, inc=1, device_id={"col": lax.rem(me + off, n)}, device_id_type=MESH)
    for off in range(1, experts):
        pl.semaphore_signal(barrier, inc=1, device_id={"expert": lax.rem(mine + off, experts)}, device_id_type=MESH)
    pl.semaphore_wait(barrier, n + experts - 2)

    def shard_copy(it, way, s, shard):
        place = full.at[it, pl.ds(pl.multiple_of(shard * rows, 8), rows)]
        return pltpu.make_async_remote_copy(
            src_ref=place, dst_ref=place, send_sem=ag_send.at[it, way, s], recv_sem=ag_recv.at[it, way, s],
            device_id={"col": me + 1 - 2 * way}, device_id_type=MESH,
        )

    def gather_step(it, t):
        for way in range(2):
            shard = me - t * (1 - 2 * way)
            after = me + 1 - 2 * way
            inside = (shard >= 0) & (shard < n)

            if t >= 1:
                @pl.when(inside)
                def _():
                    shard_copy(it, way, t - 1, shard).wait_recv()

            if t <= n - 2:
                @pl.when(inside & (after >= 0) & (after < n))
                def _():
                    shard_copy(it, way, t, shard).start()

    def gather_sent(it):
        for way in range(2):
            for s in range(n - 1):
                shard = me - s * (1 - 2 * way)
                after = me + 1 - 2 * way

                @pl.when((shard >= 0) & (shard < n) & (after >= 0) & (after < n))
                def _():
                    shard_copy(it, way, s, shard).wait_send()

    def part_copy(it, way, s, j):
        return pltpu.make_async_remote_copy(
            src_ref=part.at[j], dst_ref=landed.at[way, s], send_sem=rs_send.at[it, way, s],
            recv_sem=rs_recv.at[it, way, s], device_id={"col": me + 1 - 2 * way}, device_id_type=MESH,
        )

    def scatter_step(it, t):
        for way in range(2):
            place = me if way == 0 else n - 1 - me
            s = t - place
            j = n - 1 - s if way == 0 else s

            @pl.when((place > 0) & (s >= 0))
            def _():
                part_copy(it, way, s, j).wait_recv()
                part[j] = part[j] + landed[way, s]

            if t <= n - 2:
                @pl.when(s >= 0)
                def _():
                    part_copy(it, way, s, j).start()

    def scatter_sent(it):
        for way in range(2):
            place = me if way == 0 else n - 1 - me
            for t in range(n - 1):
                s = t - place

                @pl.when(s >= 0)
                def _():
                    part_copy(it, way, s, n - 1 - s if way == 0 else s).wait_send()

    def expert_copy(ref, kind, off):
        place = ref.at[mine]
        return pltpu.make_async_remote_copy(
            src_ref=place, dst_ref=place, send_sem=ex_send.at[kind, off - 1], recv_sem=ex_recv.at[kind, off - 1],
            device_id={"expert": lax.rem(mine + off, experts)}, device_id_type=MESH,
        )

    def expert_start(ref, kind):
        for off in range(1, experts):
            expert_copy(ref, kind, off).start()

    def expert_wait(ref, kind):
        for off in range(1, experts):
            expert_copy(ref, kind, off).wait()

    def coef_copy(it, off):
        place = d_coef.at[it, me]
        return pltpu.make_async_remote_copy(
            src_ref=place, dst_ref=place, send_sem=co_send.at[it, off - 1], recv_sem=co_recv.at[it, off - 1],
            device_id={"col": lax.rem(me + off, n)}, device_id_type=MESH,
        )

    def mix(it, c_ref, b_ref):
        for q in range(0, hl, 128):
            def add(k, total):
                return total + c_ref[mine, pl.ds(k, 1), :] * b_ref[k, :, q : q + 128]

            mixed[:, q : q + 128] = jnp.tanh(lax.fori_loop(0, k_count, add, jnp.zeros((r, 128), F32)))
        for i, piece in enumerate(pieces(mixed[...])):
            mixed_cut[it, i * r : (i + 1) * r, :] = piece

    step = rows // 4 if (rows // 4) % 16 == 0 else rows

    def project(it):
        cut = mixed_cut[it]
        gram = fold_rows(fold(contract(cut, cut, ((1,), (1,))), r), r)
        for j in range(n):
            part[j, rows : rows + r, :] = gram

        def block(i, carry):
            at = pl.ds(pl.multiple_of(i * step, 16), step)
            value = fold(contract(target[at, :], mixed_cut[it], ((1,), (1,))), r)
            j = i // (rows // step)
            part[j, pl.ds(pl.multiple_of((i - j * (rows // step)) * step, 8), step), :] = value
            return carry

        lax.fori_loop(0, d // step, block, 0)

    def absorb(it, shard):
        half = rows // 2

        def block(i, carry):
            at = pl.ds(pl.multiple_of(shard * rows + i * half, 16), half)
            cut = jnp.concatenate(pieces(full[it, at, :]), axis=1)
            gram_sum[...] += contract(cut, jnp.concatenate([target[at, :], cut], axis=1), ((0,), (0,)))
            return carry

        lax.fori_loop(0, 2, block, 0)

    def absorb_step(it, t):
        if t == 0:
            gram_sum[...] = jnp.zeros_like(gram_sum)
            absorb(it, me)
        else:
            for way in range(2):
                shard = me - t * (1 - 2 * way)

                @pl.when((shard >= 0) & (shard < n))
                def _():
                    absorb(it, shard)

    def pre_gradient(it):
        total = fold_rows(gram_sum[...], r)
        gram = fold(total[:, hl:], r)
        now = mixed[...]
        d_mixed = jnp.dot(gram, now, precision=HIGHEST, preferred_element_type=F32) - total[:, :hl]
        d_pre[it, mine] = d_mixed * scale * (1.0 - now * now)

    def loss_add(it, shard):
        def block(i, carry):
            at = pl.ds(pl.multiple_of(shard * rows + i * step, 16), step)
            one, two = pieces(full[it, at, :], 2)
            wide = jnp.concatenate([one, two, one, two], axis=1)
            upper, lower = mixed_cut[it, :r], mixed_cut[it, r : 2 * r]
            tall = jnp.concatenate([upper, upper, lower, lower], axis=0)
            residual = contract(wide, tall, ((1,), (0,))) - target[at, :].astype(F32)
            loss_sum[...] += jnp.sum((residual * residual).reshape(step // 8, 8, hl), axis=0)
            return carry

        lax.fori_loop(0, rows // step, block, 0)

    def loss_step(it, t):
        for way in range(2):
            shard = me - t * (1 - 2 * way)

            @pl.when((shard >= 0) & (shard < n))
            def _():
                loss_add(it, shard)

    def loss_close(it):
        total = loss_sum[:, 0:128]
        for q in range(128, hl, 128):
            total = total + loss_sum[:, q : q + 128]
        loss_in[mine, it * 8 : it * 8 + 8, :] = total
        loss_sum[...] = jnp.zeros_like(loss_sum)

    def combine(c_ref, it, k, q):
        total = c_ref[0, pl.ds(k, 1), :] * d_pre[it, 0, :, q : q + 128]
        for e in range(1, experts):
            total = total + c_ref[e, pl.ds(k, 1), :] * d_pre[it, e, :, q : q + 128]
        return total

    def coef_rows(it, k, q, values):
        for e in range(experts):
            row = jnp.sum(values * d_pre[it, e, :, q : q + 128], axis=0, keepdims=True)
            at = (it, me, pl.ds(e * k_count + k, 1), slice(None))
            if q == 0:
                d_coef[at] = row
            else:
                d_coef[at] = d_coef[at] + row

    def coef_sum(it):
        total = d_coef[it, 0]
        for c in range(1, n):
            total = total + d_coef[it, c]
        return jnp.broadcast_to(jnp.sum(total, axis=1, keepdims=True), total.shape)

    def factor_gradient(i):
        at = pl.ds(pl.multiple_of(i * step, 8), step)
        before = full[0, pl.ds(pl.multiple_of(me * rows + i * step, 8), step), :]
        return at, before

    loads[0].wait()
    gather_step(0, 0)
    loads[3].wait()
    expert_start(c_one, 0)
    loads[1].wait()
    mix(0, c_one, bases)
    loads[2].wait()
    project(0)
    scatter_step(0, 0)
    absorb_step(0, 0)
    for t in range(1, n):
        gather_step(0, t)
        if t < n - 1:
            scatter_step(0, t)
        absorb_step(0, t)
    pre_gradient(0)
    expert_wait(c_one, 0)
    expert_start(d_pre.at[0], 1)
    scatter_step(0, n - 1)

    def factor_one(i, carry):
        at, before = factor_gradient(i)
        gram = part[me, rows : rows + r, :]
        g = (jnp.dot(before, gram, precision=HIGHEST, preferred_element_type=F32) - part[me, at, :]) * scale
        g_one[at, :] = g
        full[1, pl.ds(pl.multiple_of(me * rows + i * step, 8), step), :] = adam_first(before, g)
        return carry

    lax.fori_loop(0, rows // step, factor_one, 0)
    gather_step(1, 0)
    scatter_sent(0)
    gather_sent(0)
    expert_wait(d_pre.at[0], 1)

    def bases_one(k, carry):
        for q in range(0, hl, 128):
            values = bases[k, :, q : q + 128]
            b_out[k, :, q : q + 128] = adam_first(values, combine(c_one, 0, k, q))
            coef_rows(0, k, q, values)
        return carry

    lax.fori_loop(0, k_count, bases_one, 0)
    d_coef[0, me, table : table + 8, :] = jnp.zeros((8, 128), F32)
    for off in range(1, n):
        coef_copy(0, off).start()
    gather_step(1, 1)
    absorb_step(1, 0)
    for off in range(1, n):
        coef_copy(0, off).wait()
    c_two[...] = adam_first(c_one[...], coef_sum(0)[:table].reshape(experts, k_count, 128))
    mix(1, c_two, b_out)
    project(1)
    scatter_step(1, 0)
    absorb_step(1, 1)
    loss_sum[...] = jnp.zeros_like(loss_sum)

    def loss_first(j, carry):
        loss_add(0, j)
        return carry

    for t in range(2, n):
        gather_step(1, t)
        if t < n - 1:
            scatter_step(1, t - 1)
            absorb_step(1, t)
            if t == 2:
                lax.fori_loop(0, n, loss_first, 0)
                loss_close(0)
                loss_add(1, me)
                loss_step(1, 1)
            loss_step(1, t)
    absorb_step(1, n - 1)
    pre_gradient(1)
    expert_start(d_pre.at[1], 2)
    scatter_step(1, n - 2)
    loss_step(1, n - 1)
    loss_close(1)
    expert_start(loss_in, 3)
    expert_wait(d_pre.at[1], 2)
    expert_wait(loss_in, 3)

    def coefs_two(k, carry):
        for q in range(0, hl, 128):
            coef_rows(1, k, q, b_out[k, :, q : q + 128])
        return carry

    lax.fori_loop(0, k_count, coefs_two, 0)
    losses = loss_in[0]
    for e in range(1, experts):
        losses = losses + loss_in[e]
    for it in range(2):
        d_coef[1, me, table + it : table + it + 1, :] = jnp.sum(losses[it * 8 : it * 8 + 8], axis=0, keepdims=True)
    d_coef[1, me, table + 2 : table + 8, :] = jnp.zeros((6, 128), F32)
    for off in range(1, n):
        coef_copy(1, off).start()

    def bases_two(k, carry):
        for q in range(0, hl, 128):
            values = b_out[k, :, q : q + 128]
            b_out[k, :, q : q + 128] = adam_second(values, combine(c_one, 0, k, q), combine(c_two, 1, k, q))
        return carry

    lax.fori_loop(0, k_count, bases_two, 0)
    scatter_step(1, n - 1)

    def factor_two(i, carry):
        at, _ = factor_gradient(i)
        before = full[1, pl.ds(pl.multiple_of(me * rows + i * step, 8), step), :]
        gram = part[me, rows : rows + r, :]
        g = (jnp.dot(before, gram, precision=HIGHEST, preferred_element_type=F32) - part[me, at, :]) * scale
        f_out[at, :] = adam_second(before, g_one[at, :], g)
        return carry

    lax.fori_loop(0, rows // step, factor_two, 0)
    for off in range(1, n):
        coef_copy(1, off).wait()
    total = coef_sum(1)
    l_out[...] = total[table : table + 8]
    first = coef_sum(0)[:table].reshape(experts, k_count, 128)
    c_two[...] = adam_second(c_two[...], first, total[:table].reshape(experts, k_count, 128))
    c_out[...] = c_two[mine]
    scatter_sent(1)
    gather_sent(1)


def shards(target_weights, factors, bases, coefficients):
    n, experts = lax.axis_size("col"), lax.axis_size("expert")
    _, d, hl = target_weights.shape
    _, rows, r = factors.shape
    k = bases.shape[0]
    anywhere = pl.BlockSpec(memory_space=pl.ANY)
    local = pl.BlockSpec(memory_space=pltpu.VMEM)
    dma = pltpu.SemaphoreType.DMA
    new_factors, new_bases, new_coef, losses = pl.pallas_call(
        functools.partial(kernel, n, experts),
        out_shape=(
            jax.ShapeDtypeStruct((rows, r), F32),
            jax.ShapeDtypeStruct(bases.shape, F32),
            jax.ShapeDtypeStruct((k, 128), F32),
            jax.ShapeDtypeStruct((8, 128), F32),
        ),
        in_specs=[anywhere, anywhere, anywhere, anywhere],
        out_specs=(local, local, local, local),
        scratch_shapes=[
            pltpu.VMEM((d, hl), BF16),
            pltpu.VMEM(bases.shape, F32),
            pltpu.VMEM((2, d, r), F32),
            pltpu.VMEM((n, rows + r, r), F32),
            pltpu.VMEM((2, n - 1, rows + r, r), F32),
            pltpu.VMEM((2, experts, r, hl), F32),
            pltpu.VMEM((experts, k, 128), F32),
            pltpu.VMEM((experts, k, 128), F32),
            pltpu.VMEM((2, n, experts * k + 8, 128), F32),
            pltpu.VMEM((experts, 16, 128), F32),
            pltpu.VMEM((rows, r), F32),
            pltpu.VMEM((3 * r, hl + 3 * r), F32),
            pltpu.VMEM((r, hl), F32),
            pltpu.VMEM((2, 3 * r, hl), BF16),
            pltpu.VMEM((8, hl), F32),
            dma((4,)),
            dma((2, 2, n - 1)),
            dma((2, 2, n - 1)),
            dma((2, 2, n - 1)),
            dma((2, 2, n - 1)),
            dma((4, experts - 1)),
            dma((4, experts - 1)),
            dma((2, n - 1)),
            dma((2, n - 1)),
        ],
        compiler_params=pltpu.CompilerParams(
            collective_id=0, has_side_effects=True, vmem_limit_bytes=66000000
        ),
    )(target_weights[0], factors[0], bases, jnp.broadcast_to(coefficients[0][:, None], (k, 128)))
    total = losses[:2, 0]
    return (new_factors[None], new_bases, new_coef[:, 0][None], total * (1.0 / (2.0 * experts * d * hl * n)))


def solution(mesh):
    return jax.shard_map(
        shards,
        mesh=mesh,
        in_specs=(
            P(("layer", "expert"), None, "col"),
            P(("layer", "expert"), "col", None),
            P("layer", None, "col"),
            P(("layer", "expert"), None),
        ),
        out_specs=(
            P(("layer", "expert"), "col", None),
            P("layer", None, "col"),
            P(("layer", "expert"), None),
            P("layer"),
        ),
        check_vma=False,
    )
```

profile of v0, /device:TPU:0, one launch (start us, length us, event | category | flops | bytes accessed | tf_op | source)
XLA Modules:
  0.0 215.1 jit_solution(11895293615971315922)
XLA Ops:
  0.6 1.3 broadcast_in_dim.11.c_in
  2.0 199.9 %shard_map.75 = (f32[1792,128]{1,0:T(8,128)}, f32[32,128,512]{2,1,0:T(8,128)}, f32[32,128]{1,0:T(8,128)}, f32[8,128]{1,0:T(8,128)}) custom-call(bf16[7168,512]{1,0:T(8,128)(2,1)} %bitcast.5, f32[1792,128]{1,0:T(8,128)} %bitcast.7, f32[32,128,512]{2,1,0:T(8,128)} %b_hbm.1, f32[32,128]{1,0:T(8,128)} %broadcast_in_dim.11.c_in), custom_call_target="tpu_custom_call" | custom-call | tf_op jit(solution)/shard_map/pallas_call | solution.py:411
  201.9 1.3 slice_reduce_fusion
  203.2 1.3 multiply_reduce_fusion
  204.5 2.2 %copy.10 = f32[1,1792,128]{2,1,0:T(8,128)} copy(f32[1,1792,128]{2,1,0:T(8,128)} %bitcast.6) | data formatting | bytes 1835008
  206.7 8.4 %copy.11 = f32[32,128,512]{2,1,0:T(8,128)} copy(f32[32,128,512]{2,1,0:T(8,128)} %get-tuple-element.17) | data formatting | bytes 16777216
where the time goes:
time: 215 us
  Pallas kernels  200 us (93%)
  local copies, waits for them, and re-layouts  13.2 us (6%)
    pallas_call x1, Pallas kernels, shards(): pl.pallas_call(functools.partial(kernel, n, experts), out_shape=(jax.Shap...  200 us
    unnamed x2, local copies, waits for them, and re-layouts  10.5 us

commit v1 on v0

v1 whole, which is shorter than its diff:
```python
import functools

import jax
import jax.numpy as jnp
from jax import lax
from jax.experimental import pallas as pl
from jax.experimental.pallas import tpu as pltpu
from jax.sharding import PartitionSpec as P

LEARN_RATE = 0.01
BETA_ONE = 0.9
BETA_TWO = 0.999
EPSILON = 0.0001
HIGHEST = lax.Precision.HIGHEST
MESH = pl.DeviceIdType.MESH
F32 = jnp.float32
BF16 = jnp.bfloat16
LAG = 3
SEMS = 16
GROUPS = 4


def adam_first(parameter, g):
    return parameter - LEARN_RATE * g / (jnp.abs(g) + EPSILON)


def adam_second(parameter, g_one, g_two):
    first = (BETA_ONE * (1.0 - BETA_ONE) * g_one + (1.0 - BETA_ONE) * g_two) * (1.0 / (1.0 - BETA_ONE**2))
    second = (
        BETA_TWO * (1.0 - BETA_TWO) * g_one * g_one + (1.0 - BETA_TWO) * g_two * g_two
    ) * (1.0 / (1.0 - BETA_TWO**2))
    return parameter - LEARN_RATE * first / (jnp.sqrt(second) + EPSILON)


def pieces(x):
    upper = x.astype(BF16)
    return upper, (x - upper.astype(F32)).astype(BF16)


def contract(a, b, dims):
    return lax.dot_general(a, b, (dims, ((), ())), preferred_element_type=F32)


def diagonal(size):
    shape = (size, 128)
    return lax.broadcasted_iota(jnp.int32, shape, 0) == lax.broadcasted_iota(jnp.int32, shape, 1)


def to_lanes(column):
    return jnp.sum(jnp.where(diagonal(column.shape[0]), column, 0.0), axis=0, keepdims=True)


def to_rows(row, size):
    held = jnp.where(diagonal(size), jnp.broadcast_to(row, (size, 128)), 0.0)
    return jnp.broadcast_to(jnp.sum(held, axis=1, keepdims=True), (size, 128))


def chunk_count(rows):
    for count in (4, 2):
        if rows % (16 * count) == 0:
            return count
    return 1


def kernel(
    n, experts, loss_scale, t_hbm, f_hbm, b_hbm, c_in, f_out, b_out, misc_out,
    target, bases, b_grad, full, part, landed, d_pre, c_one, c_two, coef_acc, message, loss_in, g_one, gram_sum,
    mixed, tall, loss_sum, gram_own, gram_in, gram_go,
    load_sem, out_sem, z_send, z_recv, gram_send, gram_recv, ex_send, ex_recv, co_send, co_recv,
):
    me = lax.axis_index("col")
    mine = lax.axis_index("expert")
    rows, r = f_hbm.shape
    d, hl = target.shape
    k_count = bases.shape[0]
    scale = 1.0 / (hl * n)
    table = experts * k_count
    block = min(table, 128)
    blocks = table // block
    chunks = chunk_count(rows)
    ch = rows // chunks
    phase = n * chunks
    group = k_count // GROUPS

    loads = [
        pltpu.make_async_copy(f_hbm, full.at[0, pl.ds(pl.multiple_of(me * rows, 16), rows)], load_sem.at[0]),
        pltpu.make_async_copy(b_hbm, bases, load_sem.at[1]),
    ]
    for j in range(n):
        at = pl.ds(j * rows, rows)
        loads.append(pltpu.make_async_copy(t_hbm.at[at], target.at[at], load_sem.at[2 + j]))
    for load in loads:
        load.start()
    barrier = pltpu.get_barrier_semaphore()
    for off in range(1, n):
        pl.semaphore_signal(barrier, inc=1, device_id={"col": lax.rem(me + off, n)}, device_id_type=MESH)
    for off in range(1, experts):
        pl.semaphore_signal(barrier, inc=1, device_id={"expert": lax.rem(mine + off, experts)}, device_id_type=MESH)
    pl.semaphore_wait(barrier, n + experts - 2)

    def place_of(way):
        return me if way == 0 else n - 1 - me

    def shard_at(way, place):
        return place if way == 0 else n - 1 - place

    def split(s):
        it = s // phase
        u = s - it * phase
        b = u // chunks
        return it, b, u - b * chunks

    def z_copy(way, s, src, dst):
        return pltpu.make_async_remote_copy(
            src_ref=src, dst_ref=dst, send_sem=z_send.at[way, s % SEMS], recv_sem=z_recv.at[way, s % SEMS],
            device_id={"col": me + 1 - 2 * way}, device_id_type=MESH,
        )

    def rows_of(shard, c):
        return pl.ds(pl.multiple_of(shard * rows + c * ch, 16), ch)

    def chunk_of(c):
        return pl.ds(pl.multiple_of(c * ch, 16), ch)

    def gather_copy(way, s, shard):
        it, b, c = split(s)
        ref = full.at[it, rows_of(shard, c)]
        return z_copy(way, s, ref, ref)

    def scatter_copy(way, s, shard):
        it, b, c = split(s)
        return z_copy(way, s, part.at[shard, chunk_of(c)], landed.at[way, b - 1, chunk_of(c)])

    def on_send(way, s, act):
        it, b, c = split(s)
        p = place_of(way)

        @pl.when((p < n - 1) & (b <= p))
        def _():
            act(gather_copy(way, s, shard_at(way, p - b)))

        @pl.when((p < n - 1) & (b > p))
        def _():
            act(scatter_copy(way, s, shard_at(way, n + p - b)))

    def arrive(way, s):
        it, b, c = split(s)
        p = place_of(way)

        @pl.when((p > 0) & (b <= p - 1))
        def _():
            gather_copy(way, s, shard_at(way, p - 1 - b)).wait_recv()

        @pl.when((p > 0) & (b > p - 1))
        def _():
            shard = shard_at(way, n + p - 1 - b)
            scatter_copy(way, s, shard).wait_recv()
            at = chunk_of(c)
            part[shard, at, :] = part[shard, at, :] + landed[way, b - 1, at, :]

    def step(s, first=False, last=False):
        if not first:
            for way in range(2):
                on_send(way, s - LAG, lambda copy: copy.wait_send())
            for way in range(2):
                arrive(way, s - LAG)
        if not last:
            for way in range(2):
                on_send(way, s, lambda copy: copy.start())

    def gram_copy(it, way):
        return pltpu.make_async_remote_copy(
            src_ref=gram_go.at[it, way], dst_ref=gram_in.at[it, way], send_sem=gram_send.at[it, way],
            recv_sem=gram_recv.at[it, way], device_id={"col": me + 1 - 2 * way}, device_id_type=MESH,
        )

    def gram_hop(it, s, start):
        for way in range(2):
            p = place_of(way)
            now = s == start + p * LAG

            @pl.when(now & (p > 0))
            def _():
                gram_copy(it, way).wait_recv()

            @pl.when(now & (p == 0) & (p < n - 1))
            def _():
                gram_go[it, way] = gram_own[...]

            @pl.when(now & (p > 0) & (p < n - 1))
            def _():
                gram_go[it, way] = gram_own[...] + gram_in[it, way]

            @pl.when(now & (p < n - 1))
            def _():
                gram_copy(it, way).start()

    def gram_close(it):
        for way in range(2):
            p = place_of(way)

            @pl.when(p > 0)
            def _():
                gram_own[...] = gram_own[...] + gram_in[it, way]

            @pl.when(p < n - 1)
            def _():
                gram_copy(it, way).wait_send()

    def expert_copy(ref, kind, off):
        place = ref.at[mine]
        return pltpu.make_async_remote_copy(
            src_ref=place, dst_ref=place, send_sem=ex_send.at[kind, off - 1], recv_sem=ex_recv.at[kind, off - 1],
            device_id={"expert": lax.rem(mine + off, experts)}, device_id_type=MESH,
        )

    def expert_start(ref, kind):
        for off in range(1, experts):
            expert_copy(ref, kind, off).start()

    def expert_wait(ref, kind):
        for off in range(1, experts):
            expert_copy(ref, kind, off).wait()

    def coef_copy(it, off):
        place = message.at[it, me]
        return pltpu.make_async_remote_copy(
            src_ref=place, dst_ref=place, send_sem=co_send.at[it, off - 1], recv_sem=co_recv.at[it, off - 1],
            device_id={"col": lax.rem(me + off, n)}, device_id_type=MESH,
        )

    def mix(c_ref):
        for q in range(0, hl, 128):
            def add(k, total):
                return total + c_ref[mine, pl.ds(k, 1), :] * bases[k, :, q : q + 128]

            value = jnp.tanh(lax.fori_loop(0, k_count, add, jnp.zeros((r, 128), F32), unroll=4))
            mixed[:, q : q + 128] = value
            upper, lower = pieces(value)
            for i in range(2):
                tall[2 * i * r : (2 * i + 1) * r, q : q + 128] = upper
                tall[(2 * i + 1) * r : (2 * i + 2) * r, q : q + 128] = lower

    def gram_local():
        cut = tall[: 2 * r, :]
        both = contract(cut, cut, ((1,), (1,)))
        both = both[:r] + both[r:]
        gram_own[...] = both[:, :r] + both[:, r:]

    def project(j):
        def one(c, carry):
            value = contract(target[rows_of(j, c), :], tall[: 2 * r, :], ((1,), (1,)))
            part[j, chunk_of(c), :] = value[:, :r] + value[:, r:]
            return carry

        lax.fori_loop(0, chunks, one, 0)

    def absorb(it, shard, c):
        at = rows_of(shard, c)
        cut = jnp.concatenate(pieces(full[it, at, :]), axis=1)
        gram_sum[...] += contract(cut, jnp.concatenate([target[at, :], cut], axis=1), ((0,), (0,)))

    def loss_add(it, shard, c):
        at = rows_of(shard, c)
        one, two = pieces(full[it, at, :])
        wide = jnp.concatenate([one, one, two, two], axis=1)
        residual = contract(wide, tall[...], ((1,), (0,))) - target[at, :].astype(F32)
        loss_sum[...] += jnp.sum((residual * residual).reshape(ch // 8, 8, hl), axis=0)

    def arrived(way, s):
        it, b, c = split(s)
        p = place_of(way)
        return (p > 0) & (b <= p - 1), shard_at(way, p - 1 - b), c

    def for_arrived(act, it, s, own):
        first, first_shard, c = arrived(0, s)
        second, second_shard, _ = arrived(1, s)

        def one(i, carry):
            valid = jnp.where(i == 0, first, jnp.where(i == 1, second, own))
            shard = jnp.where(i == 0, first_shard, jnp.where(i == 1, second_shard, me))

            @pl.when(valid)
            def _():
                act(it, shard, c)

            return carry

        lax.fori_loop(0, 3, one, 0)

    def pre_gradient(it):
        total = gram_sum[:r, :] + gram_sum[r:, :]
        gram = total[:, hl : hl + r] + total[:, hl + r :]
        now = mixed[...]
        d_mixed = jnp.dot(gram, now, precision=HIGHEST, preferred_element_type=F32) - total[:, :hl]
        d_pre[it, mine] = d_mixed * scale * (1.0 - now * now)

    def loss_close(it):
        total = loss_sum[:, 0:128]
        for q in range(128, hl, 128):
            total = total + loss_sum[:, q : q + 128]
        loss_in[mine, it * 8 : it * 8 + 8, :] = total
        loss_sum[...] = jnp.zeros_like(loss_sum)

    def combine(c_ref, it, k, q):
        total = c_ref[0, pl.ds(k, 1), :] * d_pre[it, 0, :, q : q + 128]
        for e in range(1, experts):
            total = total + c_ref[e, pl.ds(k, 1), :] * d_pre[it, e, :, q : q + 128]
        return total

    def coef_pass(it):
        def one(k, carry):
            sums = [jnp.zeros((8, 128), F32)] * experts
            for q in range(0, hl, 128):
                values = bases[k, :, q : q + 128]
                for e in range(experts):
                    held = values * d_pre[it, e, :, q : q + 128]
                    sums[e] = sums[e] + jnp.sum(held.reshape(r // 8, 8, 128), axis=0)
            for e in range(experts):
                coef_acc[pl.ds(e * k_count + k, 1), :] = jnp.sum(sums[e], axis=0, keepdims=True)
            return carry

        lax.fori_loop(0, k_count, one, 0)

    def coef_send(it, losses=None):
        message[it, me] = jnp.zeros(message.shape[2:], F32)
        for i in range(blocks):
            column = jnp.sum(coef_acc[i * block : (i + 1) * block, :], axis=1, keepdims=True)
            message[it, me, i : i + 1, :] = to_lanes(jnp.broadcast_to(column, (block, 128)))
        if losses is not None:
            for i in range(2):
                message[it, me, blocks + i : blocks + i + 1, :] = jnp.sum(
                    losses[i * 8 : i * 8 + 8], axis=0, keepdims=True
                )
        for off in range(1, n):
            coef_copy(it, off).start()

    def coef_wait(it):
        for off in range(1, n):
            coef_copy(it, off).wait()

    def message_sum(it):
        total = message[it, 0]
        for c in range(1, n):
            total = total + message[it, c]
        return total

    def coef_table(total):
        held = [to_rows(total[i : i + 1, :], block) for i in range(blocks)]
        held = held[0] if blocks == 1 else jnp.concatenate(held, axis=0)
        return held.reshape(experts, k_count, 128)

    def bases_one(g):
        def one(k, carry):
            for q in range(0, hl, 128):
                gradient = combine(c_one, 0, k, q)
                b_grad[k, :, q : q + 128] = gradient
                bases[k, :, q : q + 128] = adam_first(bases[k, :, q : q + 128], gradient)
            return carry

        lax.fori_loop(g * group, (g + 1) * group, one, 0)

    def bases_copy(g):
        at = pl.ds(g * group, group)
        return pltpu.make_async_copy(bases.at[at], b_out.at[at], out_sem.at[g])

    def bases_two(g):
        def one(k, carry):
            for q in range(0, hl, 128):
                values = bases[k, :, q : q + 128]
                bases[k, :, q : q + 128] = adam_second(values, b_grad[k, :, q : q + 128], combine(c_two, 1, k, q))
            return carry

        lax.fori_loop(g * group, (g + 1) * group, one, 0)
        bases_copy(g).start()

    def factor_gradient(it, c):
        before = full[it, rows_of(me, c), :]
        product = jnp.dot(before, gram_own[...], precision=HIGHEST, preferred_element_type=F32)
        return before, (product - part[me, chunk_of(c), :]) * scale

    def factor_one(c):
        before, g = factor_gradient(0, c)
        g_one[chunk_of(c), :] = g
        full[1, rows_of(me, c), :] = adam_first(before, g)

    def factor_copy(c):
        at = chunk_of(c)
        return pltpu.make_async_copy(g_one.at[at], f_out.at[at], out_sem.at[GROUPS + c])

    def factor_two(c):
        before, g = factor_gradient(1, c)
        at = chunk_of(c)
        g_one[at, :] = adam_second(before, g_one[at, :], g)
        factor_copy(c).start()

    loads[0].wait()
    for s in range(LAG):
        step(s, first=True)
    c_one[mine] = to_rows(c_in[...], k_count)
    expert_start(c_one, 0)
    gram_sum[...] = jnp.zeros_like(gram_sum)
    loss_sum[...] = jnp.zeros_like(loss_sum)
    loads[1].wait()
    mix(c_one)
    gram_local()
    for j in range(n):
        loads[2 + j].wait()
        project(j)
    final = phase - chunks + LAG

    def early(s, carry):
        gram_hop(0, s, LAG)
        step(s)
        own = s - LAG < chunks
        for_arrived(absorb, 0, s - LAG, own)
        for_arrived(loss_add, 0, s - LAG, own)
        return carry

    lax.fori_loop(LAG, final, early, 0)
    pre_gradient(0)
    expert_wait(c_one, 0)
    expert_start(d_pre.at[0], 1)
    gram_close(0)
    loss_close(0)
    gram_sum[...] = jnp.zeros_like(gram_sum)

    def after_first(c):
        step(final + c)
        factor_one(c)
        absorb(1, me, c)

    def base_work(i):
        if i == 0:
            expert_wait(d_pre.at[0], 1)
            coef_pass(0)
            coef_send(0)
        elif i == 1:
            for g in range(GROUPS // 2):
                bases_one(g)
        elif i == 2:
            for g in range(GROUPS // 2, GROUPS):
                bases_one(g)

    done = 0
    for c in range(chunks):
        after_first(c)
        if c >= 1 or chunks == 1:
            base_work(done)
            done += 1
    for i in range(done, 3):
        base_work(i)

    begin = phase + chunks
    for s in range(final + chunks, begin):
        step(s)
        for_arrived(absorb, 1, s - LAG, False)
    coef_wait(0)
    c_two[...] = adam_first(c_one[...], coef_table(message_sum(0)))
    mix(c_two)
    gram_local()
    for j in range(n):
        project(j)

    behind = begin - phase - LAG + 0

    def late(s, carry):
        gram_hop(1, s, begin)
        step(s)
        for_arrived(absorb, 1, s - LAG, False)
        for_arrived(loss_add, 1, s - LAG - behind, False)

        @pl.when(s - begin < chunks)
        def _():
            loss_add(1, me, s - begin)

        return carry

    lax.fori_loop(begin, phase + final, late, 0)
    pre_gradient(1)
    expert_start(d_pre.at[1], 2)
    gram_close(1)
    for s in range(phase + final - LAG - behind, phase + final - LAG):
        for_arrived(loss_add, 1, s, False)
    loss_close(1)
    expert_start(loss_in, 3)

    def after_second(c):
        step(phase + final + c, last=phase + final + c >= 2 * phase)
        factor_two(c)

    after_second(0)
    expert_wait(d_pre.at[1], 2)
    coef_pass(1)
    expert_wait(loss_in, 3)
    losses = loss_in[0]
    for e in range(1, experts):
        losses = losses + loss_in[e]
    coef_send(1, losses)
    g = 0
    for c in range(1, chunks):
        after_second(c)
        if g < GROUPS:
            bases_two(g)
            g += 1
    for i in range(g, GROUPS):
        bases_two(i)
    coef_wait(1)
    total = message_sum(1)
    c_two[...] = adam_second(c_two[...], coef_table(message_sum(0)), coef_table(total))
    misc_out[...] = jnp.zeros_like(misc_out)
    misc_out[0:1, :] = to_lanes(c_two[mine])
    for i in range(2):
        value = jnp.sum(total[blocks + i : blocks + i + 1, :], axis=1, keepdims=True) * loss_scale
        misc_out[1 + i : 2 + i, :] = jnp.broadcast_to(value, (1, 128))
    for c in range(chunks):
        factor_copy(c).wait()
    for i in range(GROUPS):
        bases_copy(i).wait()


def hand_over(b_in, f_in, b_out, f_out, b_held, f_held, sem):
    parts = sem.shape[1] - 1
    size = b_in.shape[0] // parts
    pairs = []
    for i in range(parts):
        at = pl.ds(i * size, size)
        pairs.append((b_in.at[at], b_held.at[at], b_out.at[at]))
    pairs.append((f_in, f_held, f_out))
    ins = [pltpu.make_async_copy(a, b, sem.at[0, i]) for i, (a, b, _) in enumerate(pairs)]
    outs = [pltpu.make_async_copy(b, c, sem.at[1, i]) for i, (_, b, c) in enumerate(pairs)]
    for copy in ins:
        copy.start()
    for i, copy in enumerate(outs):
        ins[i].wait()
        copy.start()
    for copy in outs:
        copy.wait()


def shards(target_weights, factors, bases, coefficients):
    n, experts = lax.axis_size("col"), lax.axis_size("expert")
    _, d, hl = target_weights.shape
    _, rows, r = factors.shape
    k = bases.shape[0]
    chunks = chunk_count(rows)
    anywhere = pl.BlockSpec(memory_space=pl.ANY)
    local = pl.BlockSpec(memory_space=pltpu.VMEM)
    dma = pltpu.SemaphoreType.DMA
    loss_scale = 1.0 / (2.0 * experts * d * hl * n)
    new_factors, new_bases, misc = pl.pallas_call(
        functools.partial(kernel, n, experts, loss_scale),
        out_shape=(
            jax.ShapeDtypeStruct((rows, r), F32),
            jax.ShapeDtypeStruct(bases.shape, F32),
            jax.ShapeDtypeStruct((8, 128), F32),
        ),
        in_specs=[anywhere, anywhere, anywhere, local],
        out_specs=(anywhere, anywhere, local),
        scratch_shapes=[
            pltpu.VMEM((d, hl), BF16),
            pltpu.VMEM(bases.shape, F32),
            pltpu.VMEM(bases.shape, F32),
            pltpu.VMEM((2, d, r), F32),
            pltpu.VMEM((n, rows, r), F32),
            pltpu.VMEM((2, n - 1, rows, r), F32),
            pltpu.VMEM((2, experts, r, hl), F32),
            pltpu.VMEM((experts, k, 128), F32),
            pltpu.VMEM((experts, k, 128), F32),
            pltpu.VMEM((experts * k, 128), F32),
            pltpu.VMEM((2, n, 8, 128), F32),
            pltpu.VMEM((experts, 16, 128), F32),
            pltpu.VMEM((rows, r), F32),
            pltpu.VMEM((2 * r, hl + 2 * r), F32),
            pltpu.VMEM((r, hl), F32),
            pltpu.VMEM((4 * r, hl), BF16),
            pltpu.VMEM((8, hl), F32),
            pltpu.VMEM((r, r), F32),
            pltpu.VMEM((2, 2, r, r), F32),
            pltpu.VMEM((2, 2, r, r), F32),
            dma((2 + n,)),
            dma((GROUPS + chunks,)),
            dma((2, SEMS)),
            dma((2, SEMS)),
            dma((2, 2)),
            dma((2, 2)),
            dma((4, experts - 1)),
            dma((4, experts - 1)),
            dma((2, n - 1)),
            dma((2, n - 1)),
        ],
        compiler_params=pltpu.CompilerParams(
            collective_id=0, has_side_effects=True, vmem_limit_bytes=66000000
        ),
    )(target_weights[0], factors[0], bases, jnp.pad(coefficients, ((0, 0), (0, 128 - k))))
    new_bases, new_factors = pl.pallas_call(
        hand_over,
        out_shape=(
            jax.ShapeDtypeStruct(bases.shape, F32),
            jax.ShapeDtypeStruct((rows, r), F32),
        ),
        in_specs=[anywhere, anywhere],
        out_specs=(anywhere, anywhere),
        scratch_shapes=[pltpu.VMEM(bases.shape, F32), pltpu.VMEM((rows, r), F32), dma((2, 9))],
        compiler_params=pltpu.CompilerParams(vmem_limit_bytes=66000000),
    )(new_bases, new_factors)
    return (new_factors[None], new_bases, misc[0:1, :k], misc[1:3, 0])


def solution(mesh):
    return jax.shard_map(
        shards,
        mesh=mesh,
        in_specs=(
            P(("layer", "expert"), None, "col"),
            P(("layer", "expert"), "col", None),
            P("layer", None, "col"),
            P(("layer", "expert"), None),
        ),
        out_specs=(
            P(("layer", "expert"), "col", None),
            P("layer", None, "col"),
            P(("layer", "expert"), None),
            P("layer"),
        ),
        check_vma=False,
    )
```

time: 215 us -> 189 us (0.88)
  Pallas kernels: 200 us -> 183 us
  local copies, waits for them, and re-layouts: 13.2 us -> 3.67 us
    pallas_call x1 -> x2, Pallas kernels: 200 us -> 183 us  [the longest x1 176 us: shards(): pl.pallas_call(functools.partial(kernel, n, experts, loss_scale), out_sha...]
    unnamed x2 -> x0, local copies, waits for them, and re-layouts: 10.5 us -> none
where the time goes in v1:
time: 189 us; the launch traced here: 188 us
  Pallas kernels  183 us (97%)
  local copies, waits for them, and re-layouts  3.67 us (2%)
    pallas_call x1, Pallas kernels, shards(): pl.pallas_call(functools.partial(kernel, n, experts, loss_scale), out_sha...  176 us
    pallas_call x1, Pallas kernels, shards(): pl.pallas_call(hand_over, out_shape=(jax.ShapeDtypeStruct(bases.shape, F3...  6.98 us

profile of v1, /device:TPU:0, one launch (start us, length us, event | category | flops | bytes accessed | tf_op | source)
XLA Modules:
  0.0 187.6 jit_solution(3383963509467475770)
XLA Ops:
  0.6 1.2 pad.4.c_in
  1.8 176.3 %shard_map.75 = (f32[1792,128]{1,0:T(8,128)}, f32[32,128,512]{2,1,0:T(8,128)}, f32[8,128]{1,0:T(8,128)}) custom-call(bf16[7168,512]{1,0:T(8,128)(2,1)} %bitcast.3, f32[1792,128]{1,0:T(8,128)} %bitcast.4, f32[32,128,512]{2,1,0:T(8,128)} %b_hbm.1, f32[1,128]{1,0:T(1,128)} %pad.4.c_in), custom_call_target="tpu_custom_call" | custom-call | tf_op jit(solution)/shard_map/pallas_call | solution.py:551
  178.2 7.0 %shard_map.76 = (f32[32,128,512]{2,1,0:T(8,128)}, f32[1792,128]{1,0:T(8,128)}) custom-call(f32[32,128,512]{2,1,0:T(8,128)} %get-tuple-element.9.b_in, f32[1792,128]{1,0:T(8,128)} %get-tuple-element.10.f_in), custom_call_target="tpu_custom_call" | custom-call | tf_op jit(solution)/shard_map/pallas_call | solution.py:596
  185.1 1.3 slice_reduce_fusion
  186.4 1.2 slice.6

commit v2 on v1

--- a/solution.py
+++ b/solution.py
@@ -15,9 +15,11 @@
 MESH = pl.DeviceIdType.MESH
 F32 = jnp.float32
 BF16 = jnp.bfloat16
+CHUNKS = 4
 LAG = 3
+VMEM_MAIN = 57000000
+VMEM_LAST = 4000000
 SEMS = 16
-GROUPS = 4
 
 
 def adam_first(parameter, g):
@@ -55,18 +57,11 @@
     return jnp.broadcast_to(jnp.sum(held, axis=1, keepdims=True), (size, 128))
 
 
-def chunk_count(rows):
-    for count in (4, 2):
-        if rows % (16 * count) == 0:
-            return count
-    return 1
-
-
 def kernel(
-    n, experts, loss_scale, t_hbm, f_hbm, b_hbm, c_in, f_out, b_out, misc_out,
-    target, bases, b_grad, full, part, landed, d_pre, c_one, c_two, coef_acc, message, loss_in, g_one, gram_sum,
-    mixed, tall, loss_sum, gram_own, gram_in, gram_go,
-    load_sem, out_sem, z_send, z_recv, gram_send, gram_recv, ex_send, ex_recv, co_send, co_recv,
+    n, experts, loss_scale, t_hbm, f_hbm, b_hbm, c_hbm, f_out, bases, misc,
+    target, b_grad, full, part, landed, d_pre, c_one, c_two, coef_acc, message, loss_in, g_one, gram_sum,
+    mixed, tall, loss_sum, gram_own, gram_in, gram_go, c_raw,
+    load_sem, z_send, z_recv, gram_send, gram_recv, ex_send, ex_recv, pre_send, pre_recv, co_send, co_recv,
 ):
     me = lax.axis_index("col")
     mine = lax.axis_index("expert")
@@ -77,18 +72,21 @@
     table = experts * k_count
     block = min(table, 128)
     blocks = table // block
-    chunks = chunk_count(rows)
+    chunks = CHUNKS
     ch = rows // chunks
     phase = n * chunks
-    group = k_count // GROUPS
+    quarters = hl // 128
+    pairs = experts // 2
+    mate = mine + 1 - 2 * lax.rem(mine, 2)
 
     loads = [
         pltpu.make_async_copy(f_hbm, full.at[0, pl.ds(pl.multiple_of(me * rows, 16), rows)], load_sem.at[0]),
         pltpu.make_async_copy(b_hbm, bases, load_sem.at[1]),
+        pltpu.make_async_copy(c_hbm, c_raw, load_sem.at[2]),
     ]
     for j in range(n):
         at = pl.ds(j * rows, rows)
-        loads.append(pltpu.make_async_copy(t_hbm.at[at], target.at[at], load_sem.at[2 + j]))
+        loads.append(pltpu.make_async_copy(t_hbm.at[at], target.at[at], load_sem.at[3 + j]))
     for load in loads:
         load.start()
     barrier = pltpu.get_barrier_semaphore()
@@ -158,15 +156,25 @@
             at = chunk_of(c)
             part[shard, at, :] = part[shard, at, :] + landed[way, b - 1, at, :]
 
-    def step(s, first=False, last=False):
-        if not first:
-            for way in range(2):
-                on_send(way, s - LAG, lambda copy: copy.wait_send())
-            for way in range(2):
-                arrive(way, s - LAG)
-        if not last:
-            for way in range(2):
-                on_send(way, s, lambda copy: copy.start())
+    def take(s):
+        for way in range(2):
+            on_send(way, s - LAG, lambda copy: copy.wait_send())
+        for way in range(2):
+            arrive(way, s - LAG)
+
+    def give(s):
+        for way in range(2):
+            on_send(way, s, lambda copy: copy.start())
+
+    def step(s):
+        take(s)
+        give(s)
+
+    def give_first(s):
+        for way in range(2):
+            @pl.when(place_of(way) < n - 1)
+            def _():
+                z_copy(way, s, f_hbm.at[chunk_of(s)], full.at[0, rows_of(me, s)]).start()
 
     def gram_copy(it, way):
         return pltpu.make_async_remote_copy(
@@ -222,6 +230,37 @@
         for off in range(1, experts):
             expert_copy(ref, kind, off).wait()
 
+    def pre_copy(it, q, e, i, target):
+        place = d_pre.at[it, e, q]
+        return pltpu.make_async_remote_copy(
+            src_ref=place, dst_ref=place, send_sem=pre_send.at[it, q, i], recv_sem=pre_recv.at[it, q, i],
+            device_id={"expert": target}, device_id_type=MESH,
+        )
+
+    def across(i):
+        return lax.rem(mine + 2 * i, experts)
+
+    def pre_start(it):
+        for q in range(quarters):
+            for i in range(1, pairs):
+                pre_copy(it, q, mine, i - 1, across(i)).start()
+            pre_copy(it, q, mine, pairs - 1, mate).start()
+
+    def pre_forward(it, q):
+        for i in range(1, pairs):
+            source = across(pairs - i)
+            pre_copy(it, q, source, i - 1, mate).wait_recv()
+            pre_copy(it, q, source, pairs - 1 + i, mate).start()
+
+    def pre_wait(it, q):
+        for i in range(1, pairs):
+            pre_copy(it, q, mine, i - 1, across(i)).wait_send()
+        pre_copy(it, q, mine, pairs - 1, mate).wait_send()
+        pre_copy(it, q, mate, pairs - 1, mate).wait_recv()
+        for i in range(1, pairs):
+            pre_copy(it, q, across(pairs - i), pairs - 1 + i, mate).wait_send()
+            pre_copy(it, q, lax.rem(mate + 2 * (pairs - i), experts), pairs - 1 + i, mate).wait_recv()
+
     def coef_copy(it, off):
         place = message.at[it, me]
         return pltpu.make_async_remote_copy(
@@ -293,7 +332,9 @@
         gram = total[:, hl : hl + r] + total[:, hl + r :]
         now = mixed[...]
         d_mixed = jnp.dot(gram, now, precision=HIGHEST, preferred_element_type=F32) - total[:, :hl]
-        d_pre[it, mine] = d_mixed * scale * (1.0 - now * now)
+        value = d_mixed * scale * (1.0 - now * now)
+        for q in range(quarters):
+            d_pre[it, mine, q] = value[:, q * 128 : (q + 1) * 128]
 
     def loss_close(it):
         total = loss_sum[:, 0:128]
@@ -303,21 +344,26 @@
         loss_sum[...] = jnp.zeros_like(loss_sum)
 
     def combine(c_ref, it, k, q):
-        total = c_ref[0, pl.ds(k, 1), :] * d_pre[it, 0, :, q : q + 128]
+        total = c_ref[0, pl.ds(k, 1), :] * d_pre[it, 0, q]
         for e in range(1, experts):
-            total = total + c_ref[e, pl.ds(k, 1), :] * d_pre[it, e, :, q : q + 128]
+            total = total + c_ref[e, pl.ds(k, 1), :] * d_pre[it, e, q]
         return total
 
-    def coef_pass(it):
+    def columns(q):
+        return slice(q * 128, (q + 1) * 128)
+
+    def coef_pass(it, which):
         def one(k, carry):
             sums = [jnp.zeros((8, 128), F32)] * experts
-            for q in range(0, hl, 128):
-                values = bases[k, :, q : q + 128]
+            for q in which:
+                values = bases[k, :, columns(q)]
                 for e in range(experts):
-                    held = values * d_pre[it, e, :, q : q + 128]
+                    held = values * d_pre[it, e, q]
                     sums[e] = sums[e] + jnp.sum(held.reshape(r // 8, 8, 128), axis=0)
             for e in range(experts):
-                coef_acc[pl.ds(e * k_count + k, 1), :] = jnp.sum(sums[e], axis=0, keepdims=True)
+                at = pl.ds(e * k_count + k, 1)
+                value = jnp.sum(sums[e], axis=0, keepdims=True)
+                coef_acc[at, :] = value if 0 in which else coef_acc[at, :] + value
             return carry
 
         lax.fori_loop(0, k_count, one, 0)
@@ -350,29 +396,23 @@
         held = held[0] if blocks == 1 else jnp.concatenate(held, axis=0)
         return held.reshape(experts, k_count, 128)
 
-    def bases_one(g):
+    def bases_one(low, high):
         def one(k, carry):
-            for q in range(0, hl, 128):
+            for q in range(quarters):
                 gradient = combine(c_one, 0, k, q)
-                b_grad[k, :, q : q + 128] = gradient
-                bases[k, :, q : q + 128] = adam_first(bases[k, :, q : q + 128], gradient)
+                b_grad[k, :, columns(q)] = gradient
+                bases[k, :, columns(q)] = adam_first(bases[k, :, columns(q)], gradient)
             return carry
 
-        lax.fori_loop(g * group, (g + 1) * group, one, 0)
-
-    def bases_copy(g):
-        at = pl.ds(g * group, group)
-        return pltpu.make_async_copy(bases.at[at], b_out.at[at], out_sem.at[g])
-
-    def bases_two(g):
+        lax.fori_loop(low, high, one, 0)
+
+    def bases_two(q):
         def one(k, carry):
-            for q in range(0, hl, 128):
-                values = bases[k, :, q : q + 128]
-                bases[k, :, q : q + 128] = adam_second(values, b_grad[k, :, q : q + 128], combine(c_two, 1, k, q))
+            values = bases[k, :, columns(q)]
+            bases[k, :, columns(q)] = adam_second(values, b_grad[k, :, columns(q)], combine(c_two, 1, k, q))
             return carry
 
-        lax.fori_loop(g * group, (g + 1) * group, one, 0)
-        bases_copy(g).start()
+        lax.fori_loop(0, k_count, one, 0, unroll=2)
 
     def factor_gradient(it, c):
         before = full[it, rows_of(me, c), :]
@@ -384,89 +424,97 @@
         g_one[chunk_of(c), :] = g
         full[1, rows_of(me, c), :] = adam_first(before, g)
 
-    def factor_copy(c):
-        at = chunk_of(c)
-        return pltpu.make_async_copy(g_one.at[at], f_out.at[at], out_sem.at[GROUPS + c])
-
     def factor_two(c):
         before, g = factor_gradient(1, c)
         at = chunk_of(c)
-        g_one[at, :] = adam_second(before, g_one[at, :], g)
-        factor_copy(c).start()
-
-    loads[0].wait()
+        f_out[at, :] = adam_second(before, g_one[at, :], g)
+
+    scope = jax.named_scope
     for s in range(LAG):
-        step(s, first=True)
-    c_one[mine] = to_rows(c_in[...], k_count)
+        give_first(s)
+    misc[...] = jnp.zeros_like(misc)
+    loads[2].wait()
+    misc[0:1, :k_count] = c_raw[...]
+    c_one[mine] = to_rows(misc[0:1, :], k_count)
     expert_start(c_one, 0)
     gram_sum[...] = jnp.zeros_like(gram_sum)
     loss_sum[...] = jnp.zeros_like(loss_sum)
-    loads[1].wait()
-    mix(c_one)
-    gram_local()
-    for j in range(n):
-        loads[2 + j].wait()
-        project(j)
+    with scope("load"):
+        loads[1].wait()
+    with scope("mix"):
+        mix(c_one)
+        gram_local()
+    with scope("project"):
+        for j in range(n):
+            loads[3 + j].wait()
+            project(j)
+    loads[0].wait()
     final = phase - chunks + LAG
 
     def early(s, carry):
         gram_hop(0, s, LAG)
-        step(s)
+        with scope("step"):
+            step(s)
         own = s - LAG < chunks
         for_arrived(absorb, 0, s - LAG, own)
         for_arrived(loss_add, 0, s - LAG, own)
         return carry
 
     lax.fori_loop(LAG, final, early, 0)
-    pre_gradient(0)
-    expert_wait(c_one, 0)
-    expert_start(d_pre.at[0], 1)
-    gram_close(0)
-    loss_close(0)
-    gram_sum[...] = jnp.zeros_like(gram_sum)
-
-    def after_first(c):
-        step(final + c)
+    with scope("pre"):
+        pre_gradient(0)
+        expert_wait(c_one, 0)
+        pre_start(0)
+        gram_close(0)
+        loss_close(0)
+        gram_sum[...] = jnp.zeros_like(gram_sum)
+
+    def base_work(i):
+        if i == 0:
+            with scope("forward"):
+                for q in range(quarters):
+                    pre_forward(0, q)
+        elif i == 1:
+            with scope("wait"):
+                for q in range(quarters):
+                    pre_wait(0, q)
+            with scope("coef"):
+                coef_pass(0, range(quarters))
+                coef_send(0)
+        elif i == 2:
+            with scope("bases"):
+                bases_one(0, k_count // 2)
+        else:
+            with scope("bases"):
+                bases_one(k_count // 2, k_count)
+
+    for c in range(chunks):
+        with scope("step"):
+            step(final + c)
         factor_one(c)
         absorb(1, me, c)
-
-    def base_work(i):
-        if i == 0:
-            expert_wait(d_pre.at[0], 1)
-            coef_pass(0)
-            coef_send(0)
-        elif i == 1:
-            for g in range(GROUPS // 2):
-                bases_one(g)
-        elif i == 2:
-            for g in range(GROUPS // 2, GROUPS):
-                bases_one(g)
-
-    done = 0
-    for c in range(chunks):
-        after_first(c)
-        if c >= 1 or chunks == 1:
-            base_work(done)
-            done += 1
-    for i in range(done, 3):
-        base_work(i)
+        base_work(c)
 
     begin = phase + chunks
+    behind = begin - phase - LAG
     for s in range(final + chunks, begin):
-        step(s)
+        with scope("step"):
+            step(s)
         for_arrived(absorb, 1, s - LAG, False)
-    coef_wait(0)
+    with scope("await"):
+        coef_wait(0)
     c_two[...] = adam_first(c_one[...], coef_table(message_sum(0)))
-    mix(c_two)
-    gram_local()
-    for j in range(n):
-        project(j)
-
-    behind = begin - phase - LAG + 0
+    with scope("mix"):
+        mix(c_two)
+        gram_local()
+    with scope("project"):
+        for j in range(n):
+            project(j)
 
     def late(s, carry):
         gram_hop(1, s, begin)
-        step(s)
+        with scope("step"):
+            step(s)
         for_arrived(absorb, 1, s - LAG, False)
         for_arrived(loss_add, 1, s - LAG - behind, False)
 
@@ -476,65 +524,79 @@
 
         return carry
 
-    lax.fori_loop(begin, phase + final, late, 0)
-    pre_gradient(1)
-    expert_start(d_pre.at[1], 2)
-    gram_close(1)
-    for s in range(phase + final - LAG - behind, phase + final - LAG):
+    end = phase + final
+    lax.fori_loop(begin, end, late, 0)
+    with scope("pre"):
+        pre_gradient(1)
+        pre_start(1)
+        gram_close(1)
+    for s in range(end - LAG - behind, end - LAG):
         for_arrived(loss_add, 1, s, False)
     loss_close(1)
-    expert_start(loss_in, 3)
-
-    def after_second(c):
-        step(phase + final + c, last=phase + final + c >= 2 * phase)
-        factor_two(c)
-
-    after_second(0)
-    expert_wait(d_pre.at[1], 2)
-    coef_pass(1)
-    expert_wait(loss_in, 3)
-    losses = loss_in[0]
-    for e in range(1, experts):
-        losses = losses + loss_in[e]
-    coef_send(1, losses)
-    g = 0
+    expert_start(loss_in, 1)
+    with scope("step"):
+        take(end)
+    factor_two(0)
+    with scope("forward"):
+        pre_forward(1, 0)
+    with scope("wait"):
+        pre_wait(1, 0)
+    with scope("coef"):
+        coef_pass(1, (0,))
+    with scope("forward"):
+        for q in range(1, quarters):
+            pre_forward(1, q)
+    with scope("bases"):
+        bases_two(0)
+    with scope("wait"):
+        for q in range(1, quarters):
+            pre_wait(1, q)
+    with scope("coef"):
+        if quarters > 1:
+            coef_pass(1, range(1, quarters))
+        expert_wait(loss_in, 1)
+        losses = loss_in[0]
+        for e in range(1, experts):
+            losses = losses + loss_in[e]
+        coef_send(1, losses)
+    give(end)
+    q = 1
     for c in range(1, chunks):
-        after_second(c)
-        if g < GROUPS:
-            bases_two(g)
-            g += 1
-    for i in range(g, GROUPS):
+        if q < quarters:
+            with scope("bases"):
+                bases_two(q)
+            q += 1
+        with scope("step"):
+            take(end + c)
+            if end + c < 2 * phase:
+                give(end + c)
+        with scope("factor"):
+            factor_two(c)
+    for i in range(q, quarters):
         bases_two(i)
-    coef_wait(1)
+    with scope("await"):
+        coef_wait(1)
     total = message_sum(1)
     c_two[...] = adam_second(c_two[...], coef_table(message_sum(0)), coef_table(total))
-    misc_out[...] = jnp.zeros_like(misc_out)
-    misc_out[0:1, :] = to_lanes(c_two[mine])
+    misc[0:1, :] = to_lanes(c_two[mine])
     for i in range(2):
         value = jnp.sum(total[blocks + i : blocks + i + 1, :], axis=1, keepdims=True) * loss_scale
-        misc_out[1 + i : 2 + i, :] = jnp.broadcast_to(value, (1, 128))
-    for c in range(chunks):
-        factor_copy(c).wait()
-    for i in range(GROUPS):
-        bases_copy(i).wait()
-
-
-def hand_over(b_in, f_in, b_out, f_out, b_held, f_held, sem):
-    parts = sem.shape[1] - 1
+        misc[1 + i : 2 + i, :] = jnp.broadcast_to(value, (1, 128))
+
+
+def hand_over(b_in, f_in, misc, b_out, f_out, c_out, l_out, sem):
+    parts = 8
     size = b_in.shape[0] // parts
-    pairs = []
+    copies = [pltpu.make_async_copy(f_in, f_out, sem.at[parts])]
     for i in range(parts):
         at = pl.ds(i * size, size)
-        pairs.append((b_in.at[at], b_held.at[at], b_out.at[at]))
-    pairs.append((f_in, f_held, f_out))
-    ins = [pltpu.make_async_copy(a, b, sem.at[0, i]) for i, (a, b, _) in enumerate(pairs)]
-    outs = [pltpu.make_async_copy(b, c, sem.at[1, i]) for i, (_, b, c) in enumerate(pairs)]
-    for copy in ins:
+        copies.append(pltpu.make_async_copy(b_in.at[at], b_out.at[at], sem.at[i]))
+    for copy in copies:
         copy.start()
-    for i, copy in enumerate(outs):
-        ins[i].wait()
-        copy.start()
-    for copy in outs:
+    c_out[...] = misc[0:1, : c_out.shape[1]]
+    for i in range(2):
+        l_out[i] = misc[1 + i, 0]
+    for copy in copies:
         copy.wait()
 
 
@@ -543,28 +605,26 @@
     _, d, hl = target_weights.shape
     _, rows, r = factors.shape
     k = bases.shape[0]
-    chunks = chunk_count(rows)
-    anywhere = pl.BlockSpec(memory_space=pl.ANY)
+    held = pl.BlockSpec(memory_space=pltpu.HBM)
     local = pl.BlockSpec(memory_space=pltpu.VMEM)
     dma = pltpu.SemaphoreType.DMA
     loss_scale = 1.0 / (2.0 * experts * d * hl * n)
     new_factors, new_bases, misc = pl.pallas_call(
         functools.partial(kernel, n, experts, loss_scale),
         out_shape=(
-            jax.ShapeDtypeStruct((rows, r), F32),
-            jax.ShapeDtypeStruct(bases.shape, F32),
-            jax.ShapeDtypeStruct((8, 128), F32),
+            pltpu.VMEM((rows, r), F32),
+            pltpu.VMEM(bases.shape, F32),
+            pltpu.VMEM((8, 128), F32),
         ),
-        in_specs=[anywhere, anywhere, anywhere, local],
-        out_specs=(anywhere, anywhere, local),
+        in_specs=[held, held, held, held],
+        out_specs=(local, local, local),
         scratch_shapes=[
             pltpu.VMEM((d, hl), BF16),
-            pltpu.VMEM(bases.shape, F32),
             pltpu.VMEM(bases.shape, F32),
             pltpu.VMEM((2, d, r), F32),
             pltpu.VMEM((n, rows, r), F32),
             pltpu.VMEM((2, n - 1, rows, r), F32),
-            pltpu.VMEM((2, experts, r, hl), F32),
+            pltpu.VMEM((2, experts, hl // 128, r, 128), F32),
             pltpu.VMEM((experts, k, 128), F32),
             pltpu.VMEM((experts, k, 128), F32),
             pltpu.VMEM((experts * k, 128), F32),
@@ -578,33 +638,37 @@
             pltpu.VMEM((r, r), F32),
             pltpu.VMEM((2, 2, r, r), F32),
             pltpu.VMEM((2, 2, r, r), F32),
-            dma((2 + n,)),
-            dma((GROUPS + chunks,)),
+            pltpu.VMEM((1, k), F32),
+            dma((3 + n,)),
             dma((2, SEMS)),
             dma((2, SEMS)),
             dma((2, 2)),
             dma((2, 2)),
-            dma((4, experts - 1)),
-            dma((4, experts - 1)),
+            dma((2, experts - 1)),
+            dma((2, experts - 1)),
+            dma((2, hl // 128, experts - 1)),
+            dma((2, hl // 128, experts - 1)),
             dma((2, n - 1)),
             dma((2, n - 1)),
         ],
         compiler_params=pltpu.CompilerParams(
-            collective_id=0, has_side_effects=True, vmem_limit_bytes=66000000
+            collective_id=0, has_side_effects=True, vmem_limit_bytes=VMEM_MAIN
         ),
-    )(target_weights[0], factors[0], bases, jnp.pad(coefficients, ((0, 0), (0, 128 - k))))
-    new_bases, new_factors = pl.pallas_call(
+    )(target_weights[0], factors[0], bases, coefficients)
+    new_bases, new_factors, new_coef, losses = pl.pallas_call(
         hand_over,
         out_shape=(
             jax.ShapeDtypeStruct(bases.shape, F32),
             jax.ShapeDtypeStruct((rows, r), F32),
+            jax.ShapeDtypeStruct((1, k), F32),
+            jax.ShapeDtypeStruct((2,), F32),
         ),
-        in_specs=[anywhere, anywhere],
-        out_specs=(anywhere, anywhere),
-        scratch_shapes=[pltpu.VMEM(bases.shape, F32), pltpu.VMEM((rows, r), F32), dma((2, 9))],
-        compiler_params=pltpu.CompilerParams(vmem_limit_bytes=66000000),
-    )(new_bases, new_factors)
-    return (new_factors[None], new_bases, misc[0:1, :k], misc[1:3, 0])
+        in_specs=[local, local, local],
+        out_specs=(held, held, local, pl.BlockSpec(memory_space=pltpu.SMEM)),
+        scratch_shapes=[dma((9,))],
+        compiler_params=pltpu.CompilerParams(vmem_limit_bytes=VMEM_LAST),
+    )(new_bases, new_factors, misc)
+    return (new_factors[None], new_bases, new_coef, losses)
 
 
 def solution(mesh):

time: 189 us -> 176 us (0.931)
  Pallas kernels: 183 us -> 176 us
  local copies, waits for them, and re-layouts: 3.67 us -> 0 us
    pallas_call x1, Pallas kernels: 176 us -> 171 us  [shards(): pl.pallas_call(functools.partial(kernel, n, experts, loss_scale), out_sha...]
    pallas_call x1, Pallas kernels: 6.98 us -> 4.2 us  [shards(): pl.pallas_call(hand_over, out_shape=(jax.ShapeDtypeStruct(bases.shape, F3...]
    slice x2 -> x0, local copies, waits for them, and re-layouts: 2.5 us -> none  [shards(): return (new_factors[None], new_bases, misc[0:1, :k], misc[1:3, 0])]
where the time goes in v2:
time: 176 us
  Pallas kernels  176 us (100%)
    pallas_call x1, Pallas kernels, shards(): pl.pallas_call(functools.partial(kernel, n, experts, loss_scale), out_sha...  171 us
    pallas_call x1, Pallas kernels, shards(): pl.pallas_call(hand_over, out_shape=(jax.ShapeDtypeStruct(bases.shape, F3...  4.2 us

profile of v2, /device:TPU:0, one launch (start us, length us, event | category | flops | bytes accessed | tf_op | source)
XLA Modules:
  0.0 176.2 jit_solution(3324827394857121184)
XLA Ops:
  0.6 171.4 %shard_map.75 = (f32[1792,128]{1,0:T(8,128)S(1)}, f32[32,128,512]{2,1,0:T(8,128)S(1)}, f32[8,128]{1,0:T(8,128)S(1)}) custom-call(bf16[7168,512]{1,0:T(8,128)(2,1)} %bitcast.3, f32[1792,128]{1,0:T(8,128)} %bitcast.4, f32[32,128,512]{2,1,0:T(8,128)} %b_hbm.1, f32[1,32]{1,0:T(1,128)} %c_hbm.1), custom_call_target="tpu_custom_call" | custom-call | tf_op jit(solution)/shard_map/pallas_call | solution.py:612
  172.0 4.2 %shard_map.76 = (f32[32,128,512]{2,1,0:T(8,128)}, f32[1792,128]{1,0:T(8,128)}, f32[1,32]{1,0:T(1,128)}, f32[2]{0:T(128)}) custom-call(f32[32,128,512]{2,1,0:T(8,128)S(1)} %get-tuple-element.11.b_in, f32[1792,128]{1,0:T(8,128)S(1)} %get-tuple-element.12.f_in, f32[8,128]{1,0:T(8,128)S(1)} %get-tuple-element.13.misc), custom_call_target="tpu_custom_call" | custom-call | tf_op jit(solution)/shard_map/pallas_call | solution.py:658

commit v3 on v2

--- a/solution.py
+++ b/solution.py
@@ -26,12 +26,16 @@
     return parameter - LEARN_RATE * g / (jnp.abs(g) + EPSILON)
 
 
-def adam_second(parameter, g_one, g_two):
-    first = (BETA_ONE * (1.0 - BETA_ONE) * g_one + (1.0 - BETA_ONE) * g_two) * (1.0 / (1.0 - BETA_ONE**2))
-    second = (
-        BETA_TWO * (1.0 - BETA_TWO) * g_one * g_one + (1.0 - BETA_TWO) * g_two * g_two
-    ) * (1.0 / (1.0 - BETA_TWO**2))
-    return parameter - LEARN_RATE * first / (jnp.sqrt(second) + EPSILON)
+ROOT_ONE = (BETA_TWO * (1.0 - BETA_TWO) / (1.0 - BETA_TWO**2)) ** 0.5
+ROOT_TWO = ((1.0 - BETA_TWO) / (1.0 - BETA_TWO**2)) ** 0.5
+RATE_ONE = LEARN_RATE * BETA_ONE * (1.0 - BETA_ONE) / (1.0 - BETA_ONE**2) / ROOT_ONE
+RATE_TWO = LEARN_RATE * (1.0 - BETA_ONE) / (1.0 - BETA_ONE**2) / ROOT_TWO
+
+
+def adam_second(parameter, h_one, h_two):
+    second = h_one * h_one + h_two * h_two
+    root = second * lax.rsqrt(jnp.maximum(second, 1e-30))
+    return parameter - (RATE_ONE * h_one + RATE_TWO * h_two) / (root + EPSILON)
 
 
 def pieces(x):
@@ -59,7 +63,7 @@
 
 def kernel(
     n, experts, loss_scale, t_hbm, f_hbm, b_hbm, c_hbm, f_out, bases, misc,
-    target, b_grad, full, part, landed, d_pre, c_one, c_two, coef_acc, message, loss_in, g_one, gram_sum,
+    target, b_grad, full, part, landed, d_pre, c_one, c_two, c_root, c_grad, coef_acc, message, loss_in, g_one, gram_sum,
     mixed, tall, loss_sum, gram_own, gram_in, gram_go, c_raw,
     load_sem, z_send, z_recv, gram_send, gram_recv, ex_send, ex_recv, pre_send, pre_recv, co_send, co_recv,
 ):
@@ -90,11 +94,14 @@
     for load in loads:
         load.start()
     barrier = pltpu.get_barrier_semaphore()
-    for off in range(1, n):
-        pl.semaphore_signal(barrier, inc=1, device_id={"col": lax.rem(me + off, n)}, device_id_type=MESH)
+    for way in range(2):
+        @pl.when((me + 1 - 2 * way >= 0) & (me + 1 - 2 * way < n))
+        def _():
+            pl.semaphore_signal(barrier, inc=1, device_id={"col": me + 1 - 2 * way}, device_id_type=MESH)
+
     for off in range(1, experts):
         pl.semaphore_signal(barrier, inc=1, device_id={"expert": lax.rem(mine + off, experts)}, device_id_type=MESH)
-    pl.semaphore_wait(barrier, n + experts - 2)
+    pl.semaphore_wait(barrier, experts - 1 + jnp.where(me > 0, 1, 0) + jnp.where(me < n - 1, 1, 0))
 
     def place_of(way):
         return me if way == 0 else n - 1 - me
@@ -400,7 +407,7 @@
         def one(k, carry):
             for q in range(quarters):
                 gradient = combine(c_one, 0, k, q)
-                b_grad[k, :, columns(q)] = gradient
+                b_grad[k, :, columns(q)] = ROOT_ONE * gradient
                 bases[k, :, columns(q)] = adam_first(bases[k, :, columns(q)], gradient)
             return carry
 
@@ -409,25 +416,26 @@
     def bases_two(q):
         def one(k, carry):
             values = bases[k, :, columns(q)]
-            bases[k, :, columns(q)] = adam_second(values, b_grad[k, :, columns(q)], combine(c_two, 1, k, q))
+            bases[k, :, columns(q)] = adam_second(values, b_grad[k, :, columns(q)], combine(c_root, 1, k, q))
             return carry
 
         lax.fori_loop(0, k_count, one, 0, unroll=2)
 
-    def factor_gradient(it, c):
-        before = full[it, rows_of(me, c), :]
-        product = jnp.dot(before, gram_own[...], precision=HIGHEST, preferred_element_type=F32)
-        return before, (product - part[me, chunk_of(c), :]) * scale
+    def factor_product(it, c):
+        return jnp.dot(
+            full[it, rows_of(me, c), :], gram_own[...], precision=HIGHEST, preferred_element_type=F32
+        )
 
     def factor_one(c):
-        before, g = factor_gradient(0, c)
-        g_one[chunk_of(c), :] = g
-        full[1, rows_of(me, c), :] = adam_first(before, g)
+        at = chunk_of(c)
+        g = (factor_product(0, c) - part[me, at, :]) * scale
+        g_one[at, :] = ROOT_ONE * g
+        full[1, rows_of(me, c), :] = adam_first(full[0, rows_of(me, c), :], g)
 
     def factor_two(c):
-        before, g = factor_gradient(1, c)
         at = chunk_of(c)
-        f_out[at, :] = adam_second(before, g_one[at, :], g)
+        g = (full[0, rows_of(me, c), :] - part[me, at, :]) * (ROOT_TWO * scale)
+        f_out[at, :] = adam_second(full[1, rows_of(me, c), :], g_one[at, :], g)
 
     scope = jax.named_scope
     for s in range(LAG):
@@ -503,7 +511,9 @@
         for_arrived(absorb, 1, s - LAG, False)
     with scope("await"):
         coef_wait(0)
-    c_two[...] = adam_first(c_one[...], coef_table(message_sum(0)))
+    c_grad[...] = coef_table(message_sum(0))
+    c_two[...] = adam_first(c_one[...], c_grad[...])
+    c_root[...] = ROOT_TWO * c_two[...]
     with scope("mix"):
         mix(c_two)
         gram_local()
@@ -530,15 +540,18 @@
         pre_gradient(1)
         pre_start(1)
         gram_close(1)
+    with scope("product"):
+        for c in range(chunks):
+            full[0, rows_of(me, c), :] = factor_product(1, c)
     for s in range(end - LAG - behind, end - LAG):
         for_arrived(loss_add, 1, s, False)
     loss_close(1)
     expert_start(loss_in, 1)
+    with scope("forward"):
+        pre_forward(1, 0)
     with scope("step"):
         take(end)
     factor_two(0)
-    with scope("forward"):
-        pre_forward(1, 0)
     with scope("wait"):
         pre_wait(1, 0)
     with scope("coef"):
@@ -560,28 +573,30 @@
             losses = losses + loss_in[e]
         coef_send(1, losses)
     give(end)
-    q = 1
-    for c in range(1, chunks):
-        if q < quarters:
-            with scope("bases"):
-                bases_two(q)
-            q += 1
-        with scope("step"):
-            take(end + c)
-            if end + c < 2 * phase:
-                give(end + c)
-        with scope("factor"):
-            factor_two(c)
-    for i in range(q, quarters):
-        bases_two(i)
+    for q in range(1, quarters):
+        with scope("bases"):
+            bases_two(q)
+        if q < chunks - 1:
+            with scope("step"):
+                take(end + q)
+            factor_two(q)
+    for c in range(max(quarters, 1), chunks - 1):
+        take(end + c)
+        factor_two(c)
     with scope("await"):
         coef_wait(1)
-    total = message_sum(1)
-    c_two[...] = adam_second(c_two[...], coef_table(message_sum(0)), coef_table(total))
-    misc[0:1, :] = to_lanes(c_two[mine])
-    for i in range(2):
-        value = jnp.sum(total[blocks + i : blocks + i + 1, :], axis=1, keepdims=True) * loss_scale
-        misc[1 + i : 2 + i, :] = jnp.broadcast_to(value, (1, 128))
+    with scope("coefs"):
+        total = message_sum(1)
+        own = pl.ds(mine * k_count, k_count)
+        coef_acc[...] = coef_table(total).reshape(table, 128)
+        misc[0:1, :] = to_lanes(adam_second(c_two[mine], ROOT_ONE * c_grad[mine], ROOT_TWO * coef_acc[own, :]))
+        for i in range(2):
+            value = jnp.sum(total[blocks + i : blocks + i + 1, :], axis=1, keepdims=True) * loss_scale
+            misc[1 + i : 2 + i, :] = jnp.broadcast_to(value, (1, 128))
+    with scope("step"):
+        take(end + chunks - 1)
+    with scope("factor"):
+        factor_two(chunks - 1)
 
 
 def hand_over(b_in, f_in, misc, b_out, f_out, c_out, l_out, sem):
@@ -625,6 +640,8 @@
             pltpu.VMEM((n, rows, r), F32),
             pltpu.VMEM((2, n - 1, rows, r), F32),
             pltpu.VMEM((2, experts, hl // 128, r, 128), F32),
+            pltpu.VMEM((experts, k, 128), F32),
+            pltpu.VMEM((experts, k, 128), F32),
             pltpu.VMEM((experts, k, 128), F32),
             pltpu.VMEM((experts, k, 128), F32),
             pltpu.VMEM((experts * k, 128), F32),

time: 176 us -> 173 us (0.983)
  Pallas kernels: 176 us -> 172 us
    pallas_call x1, Pallas kernels: 171 us -> 168 us  [shards(): pl.pallas_call(functools.partial(kernel, n, experts, loss_scale), out_sha...]
where the time goes in v3:
time: 173 us
  Pallas kernels  172 us (99%)
    pallas_call x1, Pallas kernels, shards(): pl.pallas_call(functools.partial(kernel, n, experts, loss_scale), out_sha...  168 us
    pallas_call x1, Pallas kernels, shards(): pl.pallas_call(hand_over, out_shape=(jax.ShapeDtypeStruct(bases.shape, F3...  4.2 us

profile of v3, /device:TPU:0, one launch (start us, length us, event | category | flops | bytes accessed | tf_op | source)
XLA Modules:
  0.0 172.9 jit_solution(13735069023783464937)
XLA Ops:
  0.6 168.0 %shard_map.75 = (f32[1792,128]{1,0:T(8,128)S(1)}, f32[32,128,512]{2,1,0:T(8,128)S(1)}, f32[8,128]{1,0:T(8,128)S(1)}) custom-call(bf16[7168,512]{1,0:T(8,128)(2,1)} %bitcast.3, f32[1792,128]{1,0:T(8,128)} %bitcast.4, f32[32,128,512]{2,1,0:T(8,128)} %b_hbm.1, f32[1,32]{1,0:T(1,128)} %c_hbm.1), custom_call_target="tpu_custom_call" | custom-call | tf_op jit(solution)/shard_map/pallas_call | solution.py:627
  168.7 4.2 %shard_map.76 = (f32[32,128,512]{2,1,0:T(8,128)}, f32[1792,128]{1,0:T(8,128)}, f32[1,32]{1,0:T(1,128)}, f32[2]{0:T(128)}) custom-call(f32[32,128,512]{2,1,0:T(8,128)S(1)} %get-tuple-element.11.b_in, f32[1792,128]{1,0:T(8,128)S(1)} %get-tuple-element.12.f_in, f32[8,128]{1,0:T(8,128)S(1)} %get-tuple-element.13.misc), custom_call_target="tpu_custom_call" | custom-call | tf_op jit(solution)/shard_map/pallas_call | solution.py:675

commit v4 on v3

--- a/solution.py
+++ b/solution.py
@@ -56,6 +56,35 @@
     return jnp.sum(jnp.where(diagonal(column.shape[0]), column, 0.0), axis=0, keepdims=True)
 
 
+def places(shape):
+    return lax.broadcasted_iota(jnp.int32, shape, 0), lax.broadcasted_iota(jnp.int32, shape, 1)
+
+
+def pack_symmetric(g):
+    half = g.shape[0] // 2
+    row, lane = places((half, 2 * half))
+    turned = pltpu.roll(g[half:], half, 1)
+    top = jnp.where((lane > row) & (lane < half), turned, g[:half])
+    diagonal_row = jnp.sum(jnp.where(lane == row, turned, 0.0), axis=0, keepdims=True)
+    return jnp.concatenate([top, jnp.broadcast_to(diagonal_row, (8, 2 * half))], axis=0)
+
+
+def unpack_symmetric(p):
+    half = p.shape[1] // 2
+    row, lane = places((half, 2 * half))
+    top, diagonal_row = p[:half], jnp.broadcast_to(p[half : half + 1], (half, 2 * half))
+    flipped = jnp.transpose(jnp.concatenate([top, top], axis=0))
+    upper = jnp.where((lane > row) & (lane < half), flipped[:half], top)
+    last = jnp.where(lane > row, top, jnp.where(lane < row, flipped[:half], diagonal_row))
+    lower = jnp.where(lane < half, flipped[half:], pltpu.roll(last, half, 1))
+    return jnp.concatenate([upper, lower], axis=0)
+
+
+def lane_sums(x):
+    total = jnp.sum(x, axis=(0, 1), keepdims=True)
+    return jnp.where(lax.broadcasted_iota(jnp.int32, x.shape, 0) == 0, jnp.broadcast_to(total, x.shape), 0.0)
+
+
 def to_rows(row, size):
     held = jnp.where(diagonal(size), jnp.broadcast_to(row, (size, 128)), 0.0)
     return jnp.broadcast_to(jnp.sum(held, axis=1, keepdims=True), (size, 128))
@@ -64,8 +93,8 @@
 def kernel(
     n, experts, loss_scale, t_hbm, f_hbm, b_hbm, c_hbm, f_out, bases, misc,
     target, b_grad, full, part, landed, d_pre, c_one, c_two, c_root, c_grad, coef_acc, message, loss_in, g_one, gram_sum,
-    mixed, tall, loss_sum, gram_own, gram_in, gram_go, c_raw,
-    load_sem, z_send, z_recv, gram_send, gram_recv, ex_send, ex_recv, pre_send, pre_recv, co_send, co_recv,
+    mixed, tall, loss_sum, gram, gram_packed, gram_in, gram_go, c_raw,
+    entered, load_sem, z_send, z_recv, gram_send, gram_recv, ex_send, ex_recv, pre_send, pre_recv, co_send, co_recv,
 ):
     me = lax.axis_index("col")
     mine = lax.axis_index("expert")
@@ -83,6 +112,14 @@
     pairs = experts // 2
     mate = mine + 1 - 2 * lax.rem(mine, 2)
 
+    barrier = pltpu.get_barrier_semaphore()
+
+    @pl.when(me < n - 1)
+    def _():
+        pl.semaphore_signal(barrier, inc=1, device_id={"col": me + 1}, device_id_type=MESH)
+
+    for off in range(1, experts):
+        pl.semaphore_signal(barrier, inc=1, device_id={"expert": lax.rem(mine + off, experts)}, device_id_type=MESH)
     loads = [
         pltpu.make_async_copy(f_hbm, full.at[0, pl.ds(pl.multiple_of(me * rows, 16), rows)], load_sem.at[0]),
         pltpu.make_async_copy(b_hbm, bases, load_sem.at[1]),
@@ -93,15 +130,11 @@
         loads.append(pltpu.make_async_copy(t_hbm.at[at], target.at[at], load_sem.at[3 + j]))
     for load in loads:
         load.start()
-    barrier = pltpu.get_barrier_semaphore()
-    for way in range(2):
-        @pl.when((me + 1 - 2 * way >= 0) & (me + 1 - 2 * way < n))
-        def _():
-            pl.semaphore_signal(barrier, inc=1, device_id={"col": me + 1 - 2 * way}, device_id_type=MESH)
-
-    for off in range(1, experts):
-        pl.semaphore_signal(barrier, inc=1, device_id={"expert": lax.rem(mine + off, experts)}, device_id_type=MESH)
-    pl.semaphore_wait(barrier, experts - 1 + jnp.where(me > 0, 1, 0) + jnp.where(me < n - 1, 1, 0))
+
+    @pl.when(me > 0)
+    def _():
+        pl.semaphore_wait(barrier, experts)
+        pl.semaphore_signal(entered, inc=1, device_id={"col": me - 1}, device_id_type=MESH)
 
     def place_of(way):
         return me if way == 0 else n - 1 - me
@@ -177,10 +210,12 @@
         take(s)
         give(s)
 
-    def give_first(s):
-        for way in range(2):
-            @pl.when(place_of(way) < n - 1)
-            def _():
+    def give_first(way):
+        @pl.when(place_of(way) < n - 1)
+        def _():
+            if way == 0:
+                pl.semaphore_wait(entered, 1)
+            for s in range(LAG):
                 z_copy(way, s, f_hbm.at[chunk_of(s)], full.at[0, rows_of(me, s)]).start()
 
     def gram_copy(it, way):
@@ -200,11 +235,11 @@
 
             @pl.when(now & (p == 0) & (p < n - 1))
             def _():
-                gram_go[it, way] = gram_own[...]
+                gram_go[it, way] = gram_packed[...]
 
             @pl.when(now & (p > 0) & (p < n - 1))
             def _():
-                gram_go[it, way] = gram_own[...] + gram_in[it, way]
+                gram_go[it, way] = gram_packed[...] + gram_in[it, way]
 
             @pl.when(now & (p < n - 1))
             def _():
@@ -216,11 +251,13 @@
 
             @pl.when(p > 0)
             def _():
-                gram_own[...] = gram_own[...] + gram_in[it, way]
+                gram_packed[...] = gram_packed[...] + gram_in[it, way]
 
             @pl.when(p < n - 1)
             def _():
                 gram_copy(it, way).wait_send()
+
+        gram[...] = unpack_symmetric(gram_packed[...])
 
     def expert_copy(ref, kind, off):
         place = ref.at[mine]
@@ -291,7 +328,7 @@
         cut = tall[: 2 * r, :]
         both = contract(cut, cut, ((1,), (1,)))
         both = both[:r] + both[r:]
-        gram_own[...] = both[:, :r] + both[:, r:]
+        gram_packed[...] = pack_symmetric(both[:, :r] + both[:, r:])
 
     def project(j):
         def one(c, carry):
@@ -336,9 +373,9 @@
 
     def pre_gradient(it):
         total = gram_sum[:r, :] + gram_sum[r:, :]
-        gram = total[:, hl : hl + r] + total[:, hl + r :]
+        square = total[:, hl : hl + r] + total[:, hl + r :]
         now = mixed[...]
-        d_mixed = jnp.dot(gram, now, precision=HIGHEST, preferred_element_type=F32) - total[:, :hl]
+        d_mixed = jnp.dot(square, now, precision=HIGHEST, preferred_element_type=F32) - total[:, :hl]
         value = d_mixed * scale * (1.0 - now * now)
         for q in range(quarters):
             d_pre[it, mine, q] = value[:, q * 128 : (q + 1) * 128]
@@ -381,10 +418,9 @@
             column = jnp.sum(coef_acc[i * block : (i + 1) * block, :], axis=1, keepdims=True)
             message[it, me, i : i + 1, :] = to_lanes(jnp.broadcast_to(column, (block, 128)))
         if losses is not None:
-            for i in range(2):
-                message[it, me, blocks + i : blocks + i + 1, :] = jnp.sum(
-                    losses[i * 8 : i * 8 + 8], axis=0, keepdims=True
-                )
+            message[it, me, blocks : blocks + 1, :] = to_lanes(
+                jnp.concatenate([lane_sums(losses[:8]), lane_sums(losses[8:])], axis=0)
+            )
         for off in range(1, n):
             coef_copy(it, off).start()
 
@@ -423,7 +459,7 @@
 
     def factor_product(it, c):
         return jnp.dot(
-            full[it, rows_of(me, c), :], gram_own[...], precision=HIGHEST, preferred_element_type=F32
+            full[it, rows_of(me, c), :], gram[...], precision=HIGHEST, preferred_element_type=F32
         )
 
     def factor_one(c):
@@ -438,13 +474,13 @@
         f_out[at, :] = adam_second(full[1, rows_of(me, c), :], g_one[at, :], g)
 
     scope = jax.named_scope
-    for s in range(LAG):
-        give_first(s)
+    with scope("enter"):
+        give_first(1)
+        give_first(0)
     misc[...] = jnp.zeros_like(misc)
     loads[2].wait()
     misc[0:1, :k_count] = c_raw[...]
     c_one[mine] = to_rows(misc[0:1, :], k_count)
-    expert_start(c_one, 0)
     gram_sum[...] = jnp.zeros_like(gram_sum)
     loss_sum[...] = jnp.zeros_like(loss_sum)
     with scope("load"):
@@ -456,6 +492,12 @@
         for j in range(n):
             loads[3 + j].wait()
             project(j)
+
+    @pl.when(me == 0)
+    def _():
+        pl.semaphore_wait(barrier, experts - 1)
+
+    expert_start(c_one, 0)
     loads[0].wait()
     final = phase - chunks + LAG
 
@@ -590,9 +632,7 @@
         own = pl.ds(mine * k_count, k_count)
         coef_acc[...] = coef_table(total).reshape(table, 128)
         misc[0:1, :] = to_lanes(adam_second(c_two[mine], ROOT_ONE * c_grad[mine], ROOT_TWO * coef_acc[own, :]))
-        for i in range(2):
-            value = jnp.sum(total[blocks + i : blocks + i + 1, :], axis=1, keepdims=True) * loss_scale
-            misc[1 + i : 2 + i, :] = jnp.broadcast_to(value, (1, 128))
+        misc[1:2, :] = total[blocks : blocks + 1, :] * loss_scale
     with scope("step"):
         take(end + chunks - 1)
     with scope("factor"):
@@ -610,7 +650,7 @@
         copy.start()
     c_out[...] = misc[0:1, : c_out.shape[1]]
     for i in range(2):
-        l_out[i] = misc[1 + i, 0]
+        l_out[i] = misc[1, 8 * i]
     for copy in copies:
         copy.wait()
 
@@ -645,7 +685,7 @@
             pltpu.VMEM((experts, k, 128), F32),
             pltpu.VMEM((experts, k, 128), F32),
             pltpu.VMEM((experts * k, 128), F32),
-            pltpu.VMEM((2, n, 8, 128), F32),
+            pltpu.VMEM((2, n, experts * k // min(experts * k, 128) + 1, 128), F32),
             pltpu.VMEM((experts, 16, 128), F32),
             pltpu.VMEM((rows, r), F32),
             pltpu.VMEM((2 * r, hl + 2 * r), F32),
@@ -653,9 +693,11 @@
             pltpu.VMEM((4 * r, hl), BF16),
             pltpu.VMEM((8, hl), F32),
             pltpu.VMEM((r, r), F32),
-            pltpu.VMEM((2, 2, r, r), F32),
-            pltpu.VMEM((2, 2, r, r), F32),
+            pltpu.VMEM((r // 2 + 8, r), F32),
+            pltpu.VMEM((2, 2, r // 2 + 8, r), F32),
+            pltpu.VMEM((2, 2, r // 2 + 8, r), F32),
             pltpu.VMEM((1, k), F32),
+            pltpu.SemaphoreType.REGULAR,
             dma((3 + n,)),
             dma((2, SEMS)),
             dma((2, SEMS)),

time: 173 us -> 171 us (0.988)
  no operation moved by 1% of the time
where the time goes in v4:
time: 171 us
  Pallas kernels  171 us (100%)
    pallas_call x1, Pallas kernels, shards(): pl.pallas_call(functools.partial(kernel, n, experts, loss_scale), out_sha...  166 us
    pallas_call x1, Pallas kernels, shards(): pl.pallas_call(hand_over, out_shape=(jax.ShapeDtypeStruct(bases.shape, F3...  4.2 us

profile of v4, /device:TPU:0, one launch (start us, length us, event | category | flops | bytes accessed | tf_op | source)
XLA Modules:
  0.0 171.2 jit_solution(14031949920435587316)
XLA Ops:
  0.6 166.3 %shard_map.75 = (f32[1792,128]{1,0:T(8,128)S(1)}, f32[32,128,512]{2,1,0:T(8,128)S(1)}, f32[8,128]{1,0:T(8,128)S(1)}) custom-call(bf16[7168,512]{1,0:T(8,128)(2,1)} %bitcast.3, f32[1792,128]{1,0:T(8,128)} %bitcast.4, f32[32,128,512]{2,1,0:T(8,128)} %b_hbm.1, f32[1,32]{1,0:T(1,128)} %c_hbm.1), custom_call_target="tpu_custom_call" | custom-call | tf_op jit(solution)/shard_map/pallas_call | solution.py:667
  167.0 4.2 %shard_map.76 = (f32[32,128,512]{2,1,0:T(8,128)}, f32[1792,128]{1,0:T(8,128)}, f32[1,32]{1,0:T(1,128)}, f32[2]{0:T(128)}) custom-call(f32[32,128,512]{2,1,0:T(8,128)S(1)} %get-tuple-element.11.b_in, f32[1792,128]{1,0:T(8,128)S(1)} %get-tuple-element.12.f_in, f32[8,128]{1,0:T(8,128)S(1)} %get-tuple-element.13.misc), custom_call_target="tpu_custom_call" | custom-call | tf_op jit(solution)/shard_map/pallas_call | solution.py:717

commit v5 on v4

--- a/solution.py
+++ b/solution.py
@@ -19,7 +19,6 @@
 LAG = 3
 VMEM_MAIN = 57000000
 VMEM_LAST = 4000000
-SEMS = 16
 
 
 def adam_first(parameter, g):
@@ -125,8 +124,9 @@
         pltpu.make_async_copy(b_hbm, bases, load_sem.at[1]),
         pltpu.make_async_copy(c_hbm, c_raw, load_sem.at[2]),
     ]
-    for j in range(n):
-        at = pl.ds(j * rows, rows)
+    halves = 2 if n % 2 == 0 else 1
+    for j in range(halves):
+        at = pl.ds(j * (d // halves), d // halves)
         loads.append(pltpu.make_async_copy(t_hbm.at[at], target.at[at], load_sem.at[3 + j]))
     for load in loads:
         load.start()
@@ -150,7 +150,7 @@
 
     def z_copy(way, s, src, dst):
         return pltpu.make_async_remote_copy(
-            src_ref=src, dst_ref=dst, send_sem=z_send.at[way, s % SEMS], recv_sem=z_recv.at[way, s % SEMS],
+            src_ref=src, dst_ref=dst, send_sem=z_send.at[way, s % LAG], recv_sem=z_recv.at[way, s % (2 * LAG)],
             device_id={"col": me + 1 - 2 * way}, device_id_type=MESH,
         )
 
@@ -275,9 +275,9 @@
             expert_copy(ref, kind, off).wait()
 
     def pre_copy(it, q, e, i, target):
-        place = d_pre.at[it, e, q]
+        place = d_pre.at[it, e] if it == 0 else d_pre.at[it, e, q]
         return pltpu.make_async_remote_copy(
-            src_ref=place, dst_ref=place, send_sem=pre_send.at[it, q, i], recv_sem=pre_recv.at[it, q, i],
+            src_ref=place, dst_ref=place, send_sem=pre_send.at[it + q, i], recv_sem=pre_recv.at[it + q, i],
             device_id={"expert": target}, device_id_type=MESH,
         )
 
@@ -285,7 +285,7 @@
         return lax.rem(mine + 2 * i, experts)
 
     def pre_start(it):
-        for q in range(quarters):
+        for q in range(quarters if it else 1):
             for i in range(1, pairs):
                 pre_copy(it, q, mine, i - 1, across(i)).start()
             pre_copy(it, q, mine, pairs - 1, mate).start()
@@ -490,7 +490,8 @@
         gram_local()
     with scope("project"):
         for j in range(n):
-            loads[3 + j].wait()
+            if j % (n // halves) == 0:
+                loads[3 + j // (n // halves)].wait()
             project(j)
 
     @pl.when(me == 0)
@@ -522,12 +523,10 @@
     def base_work(i):
         if i == 0:
             with scope("forward"):
-                for q in range(quarters):
-                    pre_forward(0, q)
+                pre_forward(0, 0)
         elif i == 1:
             with scope("wait"):
-                for q in range(quarters):
-                    pre_wait(0, q)
+                pre_wait(0, 0)
             with scope("coef"):
                 coef_pass(0, range(quarters))
                 coef_send(0)
@@ -698,15 +697,15 @@
             pltpu.VMEM((2, 2, r // 2 + 8, r), F32),
             pltpu.VMEM((1, k), F32),
             pltpu.SemaphoreType.REGULAR,
-            dma((3 + n,)),
-            dma((2, SEMS)),
-            dma((2, SEMS)),
+            dma((5,)),
+            dma((2, LAG)),
+            dma((2, 2 * LAG)),
             dma((2, 2)),
             dma((2, 2)),
             dma((2, experts - 1)),
             dma((2, experts - 1)),
-            dma((2, hl // 128, experts - 1)),
-            dma((2, hl // 128, experts - 1)),
+            dma((1 + hl // 128, experts - 1)),
+            dma((1 + hl // 128, experts - 1)),
             dma((2, n - 1)),
             dma((2, n - 1)),
         ],

time: 171 us -> 171 us (level)
  no operation moved by 1% of the time
where the time goes in v5:
time: 171 us
  Pallas kernels  170 us (99%)
    pallas_call x1, Pallas kernels, shards(): pl.pallas_call(functools.partial(kernel, n, experts, loss_scale), out_sha...  166 us
    pallas_call x1, Pallas kernels, shards(): pl.pallas_call(hand_over, out_shape=(jax.ShapeDtypeStruct(bases.shape, F3...  4.2 us

profile of v5, /device:TPU:0, one launch (start us, length us, event | category | flops | bytes accessed | tf_op | source)
XLA Modules:
  0.0 170.6 jit_solution(18157221018322534205)
XLA Ops:
  0.6 165.8 %shard_map.75 = (f32[1792,128]{1,0:T(8,128)S(1)}, f32[32,128,512]{2,1,0:T(8,128)S(1)}, f32[8,128]{1,0:T(8,128)S(1)}) custom-call(bf16[7168,512]{1,0:T(8,128)(2,1)} %bitcast.3, f32[1792,128]{1,0:T(8,128)} %bitcast.4, f32[32,128,512]{2,1,0:T(8,128)} %b_hbm.1, f32[1,32]{1,0:T(1,128)} %c_hbm.1), custom_call_target="tpu_custom_call" | custom-call | tf_op jit(solution)/shard_map/pallas_call | solution.py:666
  166.4 4.2 %shard_map.76 = (f32[32,128,512]{2,1,0:T(8,128)}, f32[1792,128]{1,0:T(8,128)}, f32[1,32]{1,0:T(1,128)}, f32[2]{0:T(128)}) custom-call(f32[32,128,512]{2,1,0:T(8,128)S(1)} %get-tuple-element.11.b_in, f32[1792,128]{1,0:T(8,128)S(1)} %get-tuple-element.12.f_in, f32[8,128]{1,0:T(8,128)S(1)} %get-tuple-element.13.misc), custom_call_target="tpu_custom_call" | custom-call | tf_op jit(solution)/shard_map/pallas_call | solution.py:716

commit v6 on v5

--- a/solution.py
+++ b/solution.py
@@ -93,7 +93,7 @@
     n, experts, loss_scale, t_hbm, f_hbm, b_hbm, c_hbm, f_out, bases, misc,
     target, b_grad, full, part, landed, d_pre, c_one, c_two, c_root, c_grad, coef_acc, message, loss_in, g_one, gram_sum,
     mixed, tall, loss_sum, gram, gram_packed, gram_in, gram_go, c_raw,
-    entered, load_sem, z_send, z_recv, gram_send, gram_recv, ex_send, ex_recv, pre_send, pre_recv, co_send, co_recv,
+    entered, above, known, load_sem, z_send, z_recv, gram_send, gram_recv, ex_send, ex_recv, pre_send, pre_recv, co_send, co_recv,
 ):
     me = lax.axis_index("col")
     mine = lax.axis_index("expert")
@@ -117,8 +117,16 @@
     def _():
         pl.semaphore_signal(barrier, inc=1, device_id={"col": me + 1}, device_id_type=MESH)
 
-    for off in range(1, experts):
-        pl.semaphore_signal(barrier, inc=1, device_id={"expert": lax.rem(mine + off, experts)}, device_id_type=MESH)
+    def greet_experts(semaphore):
+        for off in range(1, experts):
+            pl.semaphore_signal(
+                semaphore, inc=1, device_id={"expert": lax.rem(mine + off, experts)}, device_id_type=MESH
+            )
+
+    @pl.when(me == 0)
+    def _():
+        greet_experts(barrier)
+
     loads = [
         pltpu.make_async_copy(f_hbm, full.at[0, pl.ds(pl.multiple_of(me * rows, 16), rows)], load_sem.at[0]),
         pltpu.make_async_copy(b_hbm, bases, load_sem.at[1]),
@@ -133,7 +141,7 @@
 
     @pl.when(me > 0)
     def _():
-        pl.semaphore_wait(barrier, experts)
+        pl.semaphore_wait(barrier, 1)
         pl.semaphore_signal(entered, inc=1, device_id={"col": me - 1}, device_id_type=MESH)
 
     def place_of(way):
@@ -494,9 +502,20 @@
                 loads[3 + j // (n // halves)].wait()
             project(j)
 
-    @pl.when(me == 0)
-    def _():
-        pl.semaphore_wait(barrier, experts - 1)
+    with scope("greet"):
+        @pl.when(me == 0)
+        def _():
+            pl.semaphore_wait(barrier, experts - 1)
+
+        @pl.when(me > 0)
+        def _():
+            pl.semaphore_wait(known, 1)
+
+        @pl.when(me < n - 1)
+        def _():
+            greet_experts(above)
+            pl.semaphore_wait(above, experts - 1)
+            pl.semaphore_signal(known, inc=1, device_id={"col": me + 1}, device_id_type=MESH)
 
     expert_start(c_one, 0)
     loads[0].wait()
@@ -638,18 +657,20 @@
         factor_two(chunks - 1)
 
 
-def hand_over(b_in, f_in, misc, b_out, f_out, c_out, l_out, sem):
-    parts = 8
-    size = b_in.shape[0] // parts
-    copies = [pltpu.make_async_copy(f_in, f_out, sem.at[parts])]
-    for i in range(parts):
-        at = pl.ds(i * size, size)
-        copies.append(pltpu.make_async_copy(b_in.at[at], b_out.at[at], sem.at[i]))
-    for copy in copies:
+def hand_over(b_in, f_in, misc, b_out, f_out, c_out, l_out, c_held, l_held, sem):
+    copies = [
+        pltpu.make_async_copy(f_in, f_out, sem.at[0]),
+        pltpu.make_async_copy(b_in, b_out, sem.at[1]),
+        pltpu.make_async_copy(c_held, c_out, sem.at[2]),
+        pltpu.make_async_copy(l_held, l_out, sem.at[3]),
+    ]
+    for copy in copies[:2]:
         copy.start()
-    c_out[...] = misc[0:1, : c_out.shape[1]]
+    c_held[...] = misc[0:1, : c_out.shape[1]]
     for i in range(2):
-        l_out[i] = misc[1, 8 * i]
+        l_held[i] = misc[1, 8 * i]
+    for copy in copies[2:]:
+        copy.start()
     for copy in copies:
         copy.wait()
 
@@ -697,6 +718,8 @@
             pltpu.VMEM((2, 2, r // 2 + 8, r), F32),
             pltpu.VMEM((1, k), F32),
             pltpu.SemaphoreType.REGULAR,
+            pltpu.SemaphoreType.REGULAR,
+            pltpu.SemaphoreType.REGULAR,
             dma((5,)),
             dma((2, LAG)),
             dma((2, 2 * LAG)),
@@ -722,8 +745,8 @@
             jax.ShapeDtypeStruct((2,), F32),
         ),
         in_specs=[local, local, local],
-        out_specs=(held, held, local, pl.BlockSpec(memory_space=pltpu.SMEM)),
-        scratch_shapes=[dma((9,))],
+        out_specs=(held, held, held, held),
+        scratch_shapes=[pltpu.VMEM((1, k), F32), pltpu.SMEM((2,), F32), dma((4,))],
         compiler_params=pltpu.CompilerParams(vmem_limit_bytes=VMEM_LAST),
     )(new_bases, new_factors, misc)
     return (new_factors[None], new_bases, new_coef, losses)

time: 171 us -> 169 us (0.988)
  no operation moved by 1% of the time
where the time goes in v6:
time: 169 us
  Pallas kernels  169 us (100%)
    pallas_call x1, Pallas kernels, shards(): pl.pallas_call(functools.partial(kernel, n, experts, loss_scale), out_sha...  165 us
    pallas_call x1, Pallas kernels, shards(): pl.pallas_call(hand_over, out_shape=(jax.ShapeDtypeStruct(bases.shape, F3...  3.75 us

profile of v6, /device:TPU:0, one launch (start us, length us, event | category | flops | bytes accessed | tf_op | source)
XLA Modules:
  0.0 169.3 jit_solution(7681184498430147376)
XLA Ops:
  0.6 164.9 %shard_map.75 = (f32[1792,128]{1,0:T(8,128)S(1)}, f32[32,128,512]{2,1,0:T(8,128)S(1)}, f32[8,128]{1,0:T(8,128)S(1)}) custom-call(bf16[7168,512]{1,0:T(8,128)(2,1)} %bitcast.3, f32[1792,128]{1,0:T(8,128)} %bitcast.4, f32[32,128,512]{2,1,0:T(8,128)} %b_hbm.1, f32[1,32]{1,0:T(1,128)} %c_hbm.1), custom_call_target="tpu_custom_call" | custom-call | tf_op jit(solution)/shard_map/pallas_call | solution.py:687
  165.5 3.7 %shard_map.76 = (f32[32,128,512]{2,1,0:T(8,128)}, f32[1792,128]{1,0:T(8,128)}, f32[1,32]{1,0:T(1,128)}, f32[2]{0:T(128)}) custom-call(f32[32,128,512]{2,1,0:T(8,128)S(1)} %get-tuple-element.11.b_in, f32[1792,128]{1,0:T(8,128)S(1)} %get-tuple-element.12.f_in, f32[8,128]{1,0:T(8,128)S(1)} %get-tuple-element.13.misc), custom_call_target="tpu_custom_call" | custom-call | tf_op jit(solution)/shard_map/pallas_call | solution.py:739

commit v7 on v6

--- a/solution.py
+++ b/solution.py
@@ -228,8 +228,8 @@
 
     def gram_copy(it, way):
         return pltpu.make_async_remote_copy(
-            src_ref=gram_go.at[it, way], dst_ref=gram_in.at[it, way], send_sem=gram_send.at[it, way],
-            recv_sem=gram_recv.at[it, way], device_id={"col": me + 1 - 2 * way}, device_id_type=MESH,
+            src_ref=gram_go.at[it, way], dst_ref=gram_in.at[it, way], send_sem=gram_send.at[way],
+            recv_sem=gram_recv.at[way], device_id={"col": me + 1 - 2 * way}, device_id_type=MESH,
         )
 
     def gram_hop(it, s, start):
@@ -267,20 +267,20 @@
 
         gram[...] = unpack_symmetric(gram_packed[...])
 
-    def expert_copy(ref, kind, off):
+    def expert_copy(ref, off):
         place = ref.at[mine]
         return pltpu.make_async_remote_copy(
-            src_ref=place, dst_ref=place, send_sem=ex_send.at[kind, off - 1], recv_sem=ex_recv.at[kind, off - 1],
+            src_ref=place, dst_ref=place, send_sem=ex_send.at[off - 1], recv_sem=ex_recv.at[off - 1],
             device_id={"expert": lax.rem(mine + off, experts)}, device_id_type=MESH,
         )
 
-    def expert_start(ref, kind):
+    def expert_start(ref):
         for off in range(1, experts):
-            expert_copy(ref, kind, off).start()
-
-    def expert_wait(ref, kind):
+            expert_copy(ref, off).start()
+
+    def expert_wait(ref):
         for off in range(1, experts):
-            expert_copy(ref, kind, off).wait()
+            expert_copy(ref, off).wait()
 
     def pre_copy(it, q, e, i, target):
         place = d_pre.at[it, e] if it == 0 else d_pre.at[it, e, q]
@@ -316,7 +316,7 @@
     def coef_copy(it, off):
         place = message.at[it, me]
         return pltpu.make_async_remote_copy(
-            src_ref=place, dst_ref=place, send_sem=co_send.at[it, off - 1], recv_sem=co_recv.at[it, off - 1],
+            src_ref=place, dst_ref=place, send_sem=co_send.at[off - 1], recv_sem=co_recv.at[off - 1],
             device_id={"col": lax.rem(me + off, n)}, device_id_type=MESH,
         )
 
@@ -517,7 +517,7 @@
             pl.semaphore_wait(above, experts - 1)
             pl.semaphore_signal(known, inc=1, device_id={"col": me + 1}, device_id_type=MESH)
 
-    expert_start(c_one, 0)
+    expert_start(c_one)
     loads[0].wait()
     final = phase - chunks + LAG
 
@@ -533,7 +533,7 @@
     lax.fori_loop(LAG, final, early, 0)
     with scope("pre"):
         pre_gradient(0)
-        expert_wait(c_one, 0)
+        expert_wait(c_one)
         pre_start(0)
         gram_close(0)
         loss_close(0)
@@ -606,7 +606,7 @@
     for s in range(end - LAG - behind, end - LAG):
         for_arrived(loss_add, 1, s, False)
     loss_close(1)
-    expert_start(loss_in, 1)
+    expert_start(loss_in)
     with scope("forward"):
         pre_forward(1, 0)
     with scope("step"):
@@ -627,7 +627,7 @@
     with scope("coef"):
         if quarters > 1:
             coef_pass(1, range(1, quarters))
-        expert_wait(loss_in, 1)
+        expert_wait(loss_in)
         losses = loss_in[0]
         for e in range(1, experts):
             losses = losses + loss_in[e]
@@ -723,14 +723,14 @@
             dma((5,)),
             dma((2, LAG)),
             dma((2, 2 * LAG)),
-            dma((2, 2)),
-            dma((2, 2)),
-            dma((2, experts - 1)),
-            dma((2, experts - 1)),
+            dma((2,)),
+            dma((2,)),
+            dma((experts - 1,)),
+            dma((experts - 1,)),
             dma((1 + hl // 128, experts - 1)),
             dma((1 + hl // 128, experts - 1)),
-            dma((2, n - 1)),
-            dma((2, n - 1)),
+            dma((n - 1,)),
+            dma((n - 1,)),
         ],
         compiler_params=pltpu.CompilerParams(
             collective_id=0, has_side_effects=True, vmem_limit_bytes=VMEM_MAIN

time: 169 us -> 169 us (level)
  no operation moved by 1% of the time
where the time goes in v7:
time: 169 us
  Pallas kernels  168 us (99%)
    pallas_call x1, Pallas kernels, shards(): pl.pallas_call(functools.partial(kernel, n, experts, loss_scale), out_sha...  165 us
    pallas_call x1, Pallas kernels, shards(): pl.pallas_call(hand_over, out_shape=(jax.ShapeDtypeStruct(bases.shape, F3...  3.75 us

profile of v7, /device:TPU:0, one launch (start us, length us, event | category | flops | bytes accessed | tf_op | source)
XLA Modules:
  0.0 169.1 jit_solution(6360436582886185163)
XLA Ops:
  0.6 164.7 %shard_map.75 = (f32[1792,128]{1,0:T(8,128)S(1)}, f32[32,128,512]{2,1,0:T(8,128)S(1)}, f32[8,128]{1,0:T(8,128)S(1)}) custom-call(bf16[7168,512]{1,0:T(8,128)(2,1)} %bitcast.3, f32[1792,128]{1,0:T(8,128)} %bitcast.4, f32[32,128,512]{2,1,0:T(8,128)} %b_hbm.1, f32[1,32]{1,0:T(1,128)} %c_hbm.1), custom_call_target="tpu_custom_call" | custom-call | tf_op jit(solution)/shard_map/pallas_call | solution.py:687
  165.4 3.7 %shard_map.76 = (f32[32,128,512]{2,1,0:T(8,128)}, f32[1792,128]{1,0:T(8,128)}, f32[1,32]{1,0:T(1,128)}, f32[2]{0:T(128)}) custom-call(f32[32,128,512]{2,1,0:T(8,128)S(1)} %get-tuple-element.11.b_in, f32[1792,128]{1,0:T(8,128)S(1)} %get-tuple-element.12.f_in, f32[8,128]{1,0:T(8,128)S(1)} %get-tuple-element.13.misc), custom_call_target="tpu_custom_call" | custom-call | tf_op jit(solution)/shard_map/pallas_call | solution.py:739

commit v8 on v7

--- a/solution.py
+++ b/solution.py
@@ -117,6 +117,11 @@
     def _():
         pl.semaphore_signal(barrier, inc=1, device_id={"col": me + 1}, device_id_type=MESH)
 
+    @pl.when(me > 0)
+    def _():
+        pl.semaphore_wait(barrier, 1)
+        pl.semaphore_signal(entered, inc=1, device_id={"col": me - 1}, device_id_type=MESH)
+
     def greet_experts(semaphore):
         for off in range(1, experts):
             pl.semaphore_signal(
@@ -136,13 +141,6 @@
     for j in range(halves):
         at = pl.ds(j * (d // halves), d // halves)
         loads.append(pltpu.make_async_copy(t_hbm.at[at], target.at[at], load_sem.at[3 + j]))
-    for load in loads:
-        load.start()
-
-    @pl.when(me > 0)
-    def _():
-        pl.semaphore_wait(barrier, 1)
-        pl.semaphore_signal(entered, inc=1, device_id={"col": me - 1}, device_id_type=MESH)
 
     def place_of(way):
         return me if way == 0 else n - 1 - me
@@ -484,6 +482,8 @@
     scope = jax.named_scope
     with scope("enter"):
         give_first(1)
+        for load in loads:
+            load.start()
         give_first(0)
     misc[...] = jnp.zeros_like(misc)
     loads[2].wait()
@@ -651,10 +651,14 @@
         coef_acc[...] = coef_table(total).reshape(table, 128)
         misc[0:1, :] = to_lanes(adam_second(c_two[mine], ROOT_ONE * c_grad[mine], ROOT_TWO * coef_acc[own, :]))
         misc[1:2, :] = total[blocks : blocks + 1, :] * loss_scale
+    last = end + chunks - 1 - LAG
     with scope("step"):
-        take(end + chunks - 1)
+        for way in range(2):
+            arrive(way, last)
     with scope("factor"):
         factor_two(chunks - 1)
+    for way in range(2):
+        on_send(way, last, lambda copy: copy.wait_send())
 
 
 def hand_over(b_in, f_in, misc, b_out, f_out, c_out, l_out, c_held, l_held, sem):

time: 169 us -> 169 us (level)
  no operation moved by 1% of the time
where the time goes in v8:
time: 169 us
  Pallas kernels  168 us (99%)
    pallas_call x1, Pallas kernels, shards(): pl.pallas_call(functools.partial(kernel, n, experts, loss_scale), out_sha...  165 us
    pallas_call x1, Pallas kernels, shards(): pl.pallas_call(hand_over, out_shape=(jax.ShapeDtypeStruct(bases.shape, F3...  3.75 us

profile of v8, /device:TPU:0, one launch (start us, length us, event | category | flops | bytes accessed | tf_op | source)
XLA Modules:
  0.0 169.1 jit_solution(10795869749766609264)
XLA Ops:
  0.6 164.7 %shard_map.75 = (f32[1792,128]{1,0:T(8,128)S(1)}, f32[32,128,512]{2,1,0:T(8,128)S(1)}, f32[8,128]{1,0:T(8,128)S(1)}) custom-call(bf16[7168,512]{1,0:T(8,128)(2,1)} %bitcast.3, f32[1792,128]{1,0:T(8,128)} %bitcast.4, f32[32,128,512]{2,1,0:T(8,128)} %b_hbm.1, f32[1,32]{1,0:T(1,128)} %c_hbm.1), custom_call_target="tpu_custom_call" | custom-call | tf_op jit(solution)/shard_map/pallas_call | solution.py:691
  165.4 3.7 %shard_map.76 = (f32[32,128,512]{2,1,0:T(8,128)}, f32[1792,128]{1,0:T(8,128)}, f32[1,32]{1,0:T(1,128)}, f32[2]{0:T(128)}) custom-call(f32[32,128,512]{2,1,0:T(8,128)S(1)} %get-tuple-element.11.b_in, f32[1792,128]{1,0:T(8,128)S(1)} %get-tuple-element.12.f_in, f32[8,128]{1,0:T(8,128)S(1)} %get-tuple-element.13.misc), custom_call_target="tpu_custom_call" | custom-call | tf_op jit(solution)/shard_map/pallas_call | solution.py:743

commit v9 on v7

--- a/solution.py
+++ b/solution.py
@@ -108,6 +108,7 @@
     ch = rows // chunks
     phase = n * chunks
     quarters = hl // 128
+    width = 2 if quarters % 2 == 0 else 1
     pairs = experts // 2
     mate = mine + 1 - 2 * lax.rem(mine, 2)
 
@@ -283,7 +284,7 @@
             expert_copy(ref, off).wait()
 
     def pre_copy(it, q, e, i, target):
-        place = d_pre.at[it, e] if it == 0 else d_pre.at[it, e, q]
+        place = d_pre.at[it, e] if it == 0 else d_pre.at[it, e, pl.ds(q * width, width)]
         return pltpu.make_async_remote_copy(
             src_ref=place, dst_ref=place, send_sem=pre_send.at[it + q, i], recv_sem=pre_recv.at[it + q, i],
             device_id={"expert": target}, device_id_type=MESH,
@@ -293,7 +294,7 @@
         return lax.rem(mine + 2 * i, experts)
 
     def pre_start(it):
-        for q in range(quarters if it else 1):
+        for q in range(quarters // width if it else 1):
             for i in range(1, pairs):
                 pre_copy(it, q, mine, i - 1, across(i)).start()
             pre_copy(it, q, mine, pairs - 1, mate).start()
@@ -615,18 +616,18 @@
     with scope("wait"):
         pre_wait(1, 0)
     with scope("coef"):
-        coef_pass(1, (0,))
+        coef_pass(1, range(width))
     with scope("forward"):
-        for q in range(1, quarters):
+        for q in range(1, quarters // width):
             pre_forward(1, q)
     with scope("bases"):
         bases_two(0)
     with scope("wait"):
-        for q in range(1, quarters):
+        for q in range(1, quarters // width):
             pre_wait(1, q)
     with scope("coef"):
-        if quarters > 1:
-            coef_pass(1, range(1, quarters))
+        if quarters > width:
+            coef_pass(1, range(width, quarters))
         expert_wait(loss_in)
         losses = loss_in[0]
         for e in range(1, experts):
@@ -727,8 +728,8 @@
             dma((2,)),
             dma((experts - 1,)),
             dma((experts - 1,)),
-            dma((1 + hl // 128, experts - 1)),
-            dma((1 + hl // 128, experts - 1)),
+            dma((1 + hl // 128 // (2 if hl % 256 == 0 else 1), experts - 1)),
+            dma((1 + hl // 128 // (2 if hl % 256 == 0 else 1), experts - 1)),
             dma((n - 1,)),
             dma((n - 1,)),
         ],

time: 169 us -> 170 us (level)
  no operation moved by 1% of the time
where the time goes in v9:
time: 170 us
  Pallas kernels  169 us (99%)
    pallas_call x1, Pallas kernels, shards(): pl.pallas_call(functools.partial(kernel, n, experts, loss_scale), out_sha...  165 us
    pallas_call x1, Pallas kernels, shards(): pl.pallas_call(hand_over, out_shape=(jax.ShapeDtypeStruct(bases.shape, F3...  3.75 us

profile of v9, /device:TPU:0, one launch (start us, length us, event | category | flops | bytes accessed | tf_op | source)
XLA Modules:
  0.0 169.8 jit_solution(5271737210932953361)
XLA Ops:
  0.6 165.4 %shard_map.75 = (f32[1792,128]{1,0:T(8,128)S(1)}, f32[32,128,512]{2,1,0:T(8,128)S(1)}, f32[8,128]{1,0:T(8,128)S(1)}) custom-call(bf16[7168,512]{1,0:T(8,128)(2,1)} %bitcast.3, f32[1792,128]{1,0:T(8,128)} %bitcast.4, f32[32,128,512]{2,1,0:T(8,128)} %b_hbm.1, f32[1,32]{1,0:T(1,128)} %c_hbm.1), custom_call_target="tpu_custom_call" | custom-call | tf_op jit(solution)/shard_map/pallas_call | solution.py:688
  166.0 3.7 %shard_map.76 = (f32[32,128,512]{2,1,0:T(8,128)}, f32[1792,128]{1,0:T(8,128)}, f32[1,32]{1,0:T(1,128)}, f32[2]{0:T(128)}) custom-call(f32[32,128,512]{2,1,0:T(8,128)S(1)} %get-tuple-element.11.b_in, f32[1792,128]{1,0:T(8,128)S(1)} %get-tuple-element.12.f_in, f32[8,128]{1,0:T(8,128)S(1)} %get-tuple-element.13.misc), custom_call_target="tpu_custom_call" | custom-call | tf_op jit(solution)/shard_map/pallas_call | solution.py:740
